TPU v7x, 512 devices: a whole 4x8x8 slice. The times are simulated.
512 devices in a mesh: blk: 32 (over x_lo, y, core), tm: 16 (over z, x_hi).
Axes of the slice: x: 4 (x_hi: 2, x_lo: 2; x = x_hi * 2 + x_lo), y: 8, z: 8, core: 2. Of those that a mesh axis runs over, the one named last changes fastest.
Arguments:
- clips: bfloat16 [32, 32, 16, 36, 256], P('blk', 'tm'), may hold values from -6 to 6
- cotangent: bfloat16 [32, 32, 16, 36, 256], P('blk', 'tm'), may hold values from -6 to 6
- conv_master: float32 [3072, 256], P('blk'), may hold values from -0.125 to 0.125
- first_moment: float32 [3072, 256], P('blk'), may hold values from -3 to 3
- second_moment: float32 [3072, 256], P('blk'), may hold values from 0.1 to 100
- norm_gain: float32 [256], replicated, may hold values from 0.5 to 1.5
- norm_bias: float32 [256], replicated, may hold values from -3 to 3
Outputs:
- block_out: bfloat16 [32, 32, 16, 36, 256], P('blk', 'tm')
- input_grad: bfloat16 [32, 32, 16, 36, 256], P('blk', 'tm')
- new_master: float32 [3072, 256], P('blk')
- new_first: float32 [3072, 256], P('blk')
- new_second: float32 [3072, 256], P('blk')
- norm_grads: float32 [2, 256], replicated
All inputs are finite; a program needn't handle non-finite values.
Results may differ from a plain program's by a relative error of at most 0.0063.
Values may be sent and summed in bfloat16 or wider, within the bound.
A program may use at most 64 MiB of HBM per device.

v0:
```python
import jax
import jax.numpy as jnp
from jax import lax
from jax.sharding import PartitionSpec as P

GROUPS = 32


beta_one = 0.9
beta_two = 0.999
learn_rate = 0.003
adam_eps = 1e-08
bias_first = 1.0 - 0.9**10
bias_second = 1.0 - 0.999**10


def extended(block, sides, width):
    for axis, dim in sides:
        count = lax.axis_size(axis)
        forward = [(i, i + 1) for i in range(count - 1)]
        backward = [(target, source) for source, target in forward]
        low = lax.ppermute(
            lax.slice_in_dim(block, block.shape[dim] - width, None, axis=dim), axis, forward
        )
        high = lax.ppermute(lax.slice_in_dim(block, 0, width, axis=dim), axis, backward)
        block = jnp.concatenate([low, block, high], axis=dim)
    return block


def norm_act(field, gain, bias):
    shape = field.shape
    grouped = field.reshape(shape[:-3] + (shape[-3] * shape[-2], GROUPS, shape[-1] // GROUPS))
    center = jnp.mean(grouped, axis=(-3, -1), keepdims=True)
    spread = jnp.mean((grouped - center) ** 2, axis=(-3, -1), keepdims=True)
    normed = ((grouped - center) * lax.rsqrt(spread + 1e-05)).reshape(shape)
    return jax.nn.silu(normed * gain + bias)


def adam_update(gradient, master, first, second):
    new_first = beta_one * first + (1.0 - beta_one) * gradient
    new_second = beta_two * second + (1.0 - beta_two) * gradient * gradient
    update = new_first / bias_first / (jnp.sqrt(new_second / bias_second) + adam_eps)
    return (master - learn_rate * update, new_first, new_second)


def shards(clips, cotangent, conv_master, first_moment, second_moment, norm_gain, norm_bias):
    f32 = jnp.float32
    frames, height, width, channels = (
        clips.shape[1],
        clips.shape[2],
        clips.shape[3],
        clips.shape[4],
    )
    weights = lax.all_gather(conv_master.astype(jnp.bfloat16), "blk", axis=0, tiled=True)
    inputs32 = clips.astype(f32)
    act32, pullback = jax.vjp(norm_act, inputs32, norm_gain, norm_bias)
    act = act32.astype(jnp.bfloat16)
    act_padded = jnp.pad(act, ((0, 0), (0, 0), (1, 1), (1, 1), (0, 0)))
    space32 = jnp.zeros(clips.shape, f32)
    for row_tap in range(3):
        for col_tap in range(3):
            tap_index = 3 * row_tap + col_tap
            window = act_padded[:, :, row_tap : row_tap + height, col_tap : col_tap + width, :]
            tap = weights[tap_index * channels : (tap_index + 1) * channels]
            space32 = space32 + jnp.einsum(
                "bfhwc,cd->bfhwd", window, tap, preferred_element_type=f32
            )
    space = space32.astype(jnp.bfloat16)
    space_padded = extended(space, (("tm", 1),), 1)
    temporal = jnp.zeros(clips.shape, f32)
    for frame_tap in range(3):
        tap = weights[(9 + frame_tap) * channels : (10 + frame_tap) * channels]
        temporal = temporal + jnp.einsum(
            "bfhwc,cd->bfhwd",
            space_padded[:, frame_tap : frame_tap + frames],
            tap,
            preferred_element_type=f32,
        )
    block_out = (inputs32 + temporal).astype(jnp.bfloat16)
    back_weights = lax.all_gather(conv_master.astype(jnp.bfloat16), "blk", axis=0, tiled=True)
    grad_padded = extended(cotangent, (("tm", 1),), 1)
    space_grad32 = jnp.zeros(clips.shape, f32)
    temporal_grads = []
    for frame_tap in range(3):
        tap = back_weights[(9 + frame_tap) * channels : (10 + frame_tap) * channels]
        space_grad32 = space_grad32 + jnp.einsum(
            "bfhwd,cd->bfhwc",
            grad_padded[:, 2 - frame_tap : 2 - frame_tap + frames],
            tap,
            preferred_element_type=f32,
        )
        temporal_grads.append(
            jnp.einsum(
                "bfhwc,bfhwd->cd",
                space_padded[:, frame_tap : frame_tap + frames],
                cotangent,
                preferred_element_type=f32,
            )
        )
    space_grad = space_grad32.astype(jnp.bfloat16)
    sgrad_padded = jnp.pad(space_grad, ((0, 0), (0, 0), (1, 1), (1, 1), (0, 0)))
    act_grad = jnp.zeros(clips.shape, f32)
    spatial_grads = []
    for row_tap in range(3):
        for col_tap in range(3):
            tap_index = 3 * row_tap + col_tap
            tap = back_weights[tap_index * channels : (tap_index + 1) * channels]
            window = act_padded[:, :, row_tap : row_tap + height, col_tap : col_tap + width, :]
            spatial_grads.append(
                jnp.einsum("bfhwc,bfhwd->cd", window, space_grad, preferred_element_type=f32)
            )
            back_window = sgrad_padded[
                :, :, 2 - row_tap : 2 - row_tap + height, 2 - col_tap : 2 - col_tap + width, :
            ]
            act_grad = act_grad + jnp.einsum(
                "bfhwd,cd->bfhwc", back_window, tap, preferred_element_type=f32
            )
    input_term, gain_grad, bias_grad = pullback(act_grad)
    input_grad = (cotangent.astype(f32) + input_term).astype(jnp.bfloat16)
    local_gradient = jnp.concatenate(spatial_grads + temporal_grads, axis=0)
    norm_grads = lax.psum(jnp.stack([gain_grad, bias_grad]), ("blk", "tm"))
    row_block = lax.psum_scatter(local_gradient, "blk", scatter_dimension=0, tiled=True)
    gradient = lax.psum(row_block, "tm")
    new_master, new_first, new_second = adam_update(
        gradient, conv_master, first_moment, second_moment
    )
    return (block_out, input_grad, new_master, new_first, new_second, norm_grads)


def solution(mesh):
    placed = (
        P("blk", "tm", None, None, None),
        P("blk", "tm", None, None, None),
        P("blk", None),
        P("blk", None),
        P("blk", None),
        P(),
        P(),
    )
    return jax.shard_map(
        shards,
        mesh=mesh,
        in_specs=placed,
        out_specs=(
            P("blk", "tm", None, None, None),
            P("blk", "tm", None, None, None),
            P("blk", None),
            P("blk", None),
            P("blk", None),
            P(),
        ),
        check_vma=False,
    )
```

profile of v0, /device:TPU:8, one launch (start us, length us, event | category | flops | bytes accessed | tf_op | source)
XLA Modules:
  0.0 426.8 jit_solution(4757618439813596500)
XLA Ops:
  7.2 1.5 convert_element_type.38
  8.8 1.3 copy.26
  10.1 0.8 fusion.179
  10.9 4.9 %collective-permute-start.3 = (bf16[1,1,16,36,256]{4,3,2,1,0:T(8,128)(2,1)S(1)}, bf16[1,1,16,36,256]{4,3,2,1,0:T(8,128)(2,1)S(1)}, u32[]{:S(2)}, u32[]{:S(2)}) collective-permute-start(bf16[1,1,16,36,256]{4,3,2,1,0:T(8,128)(2,1)S(1)} %get-tuple-element.25), channel_id=1, source_target_pairs={{0,1},{1,2},{2,3},{3,4},{4,5},{5,6},{6,7},{7,8},{8,9},{9,10},{10,1... | collective-permute-start | bytes 884744 | tf_op jit(solution)/shard_map/ppermute | solution.py:22
  15.8 1.3 collective-permute-start.2
  18.3 11.4 %collective-permute-done.3 = bf16[1,1,16,36,256]{4,3,2,1,0:T(8,128)(2,1)S(1)} collective-permute-done((bf16[1,1,16,36,256]{4,3,2,1,0:T(8,128)(2,1)S(1)}, bf16[1,1,16,36,256]{4,3,2,1,0:T(8,128)(2,1)S(1)}, u32[]{:S(2)}, u32[]{:S(2)}) %collective-permute-start.3) | collective-permute-done | bytes 294944 | tf_op jit(solution)/shard_map/ppermute | solution.py:22
  29.8 0.7 copy-done.12
  30.5 50.4 %all-gather.2.cloned.1.call-done = bf16[3072,256]{1,0:T(8,128)(2,1)} async-done(((bf16[96,256]{1,0:T(8,128)(2,1)}), bf16[3072,256]{1,0:T(8,128)(2,1)}) %all-gather.2.cloned.1.call-update) | async-done | bytes 1572880 | tf_op jit(solution)/shard_map/all_gather | solution.py:54
  80.9 1.5 fusion.51
  82.5 0.4 fusion.114
  82.9 1.4 fusion.9
  84.3 0.4 fusion.66
  85.1 0.4 convolution_add_fusion.6
  85.5 0.4 convolution_add_fusion.5
  86.3 0.4 convolution_add_fusion.3
  86.7 0.4 convolution_add_fusion.2
  87.8 1.2 fusion.26
  89.0 1.1 copy-done.5
  90.1 0.5 fusion.37
  91.7 3.0 fusion.14
  94.7 1.1 fusion.49
  95.8 1.1 fusion.48
  96.9 1.1 fusion.47
  98.0 1.1 fusion.46
  99.1 1.1 fusion.45
  100.2 1.1 fusion.44
  101.3 1.1 fusion.43
  103.5 0.4 convolution_add_fusion.15
  105.0 0.5 convolution_add_fusion.11
  106.0 5.0 %collective-permute-start = (bf16[1,1,16,36,256]{4,3,2,1,0:T(8,128)(2,1)S(1)}, bf16[1,1,16,36,256]{4,3,2,1,0:T(8,128)(2,1)S(1)}, u32[]{:S(2)}, u32[]{:S(2)}) collective-permute-start(bf16[1,1,16,36,256]{4,3,2,1,0:T(8,128)(2,1)S(1)} %get-tuple-element.26), channel_id=1, source_target_pairs={{0,1},{1,2},{2,3},{3,4},{4,5},{5,6},{6,7},{7,8},{8,9},{9,10},{10,1... | collective-permute-start | bytes 884744 | tf_op jit(solution)/shard_map/ppermute | solution.py:22
  111.0 1.1 fusion.42
  112.1 1.4 collective-permute-start.1
  113.5 1.1 fusion.41
  114.6 10.7 %collective-permute-done = bf16[1,1,16,36,256]{4,3,2,1,0:T(8,128)(2,1)S(1)} collective-permute-done((bf16[1,1,16,36,256]{4,3,2,1,0:T(8,128)(2,1)S(1)}, bf16[1,1,16,36,256]{4,3,2,1,0:T(8,128)(2,1)S(1)}, u32[]{:S(2)}, u32[]{:S(2)}) %collective-permute-start) | collective-permute-done | bytes 294944 | tf_op jit(solution)/shard_map/ppermute | solution.py:22
  125.3 1.2 fusion.40
  126.5 1.1 fusion.39
  127.7 0.7 copy-done.10
  128.4 1.2 fusion.38
  129.7 1.0 copy-done.6
  130.7 0.9 copy.36
  131.7 98.4 %psum.15 = f32[2,256]{1,0:T(2,128)} all-reduce(f32[2,256]{1,0:T(2,128)S(1)} %pad_maximum_fusion.4), channel_id=1, replica_groups=mesh['blk'=32,'tm'=16] {'blk','tm'}, use_global_device_ids=true, to_apply=%region_14.15 | all-reduce | flops 512 | bytes 4096 | tf_op jit(solution)/shard_map/psum | solution.py:121
  230.1 1.4 fusion.129
  231.6 1.4 fusion.127
  233.0 19.1 %reduce-scatter.2.cloned.1.call-done = f32[96,256]{1,0:T(8,128)} async-done(((f32[3072,256]{1,0:T(8,128)}), f32[96,256]{1,0:T(8,128)}) %reduce-scatter.2.cloned.1.call-update) | async-done | bytes 98320 | tf_op jit(solution)/shard_map/reduce_scatter | solution.py:122
  252.1 2.2 fusion.11
  254.4 0.9 copy.35
  255.3 163.4 %all-reduce.4.cloned.1.call-done = f32[96,256]{1,0:T(8,128)} async-done(((f32[96,256]{1,0:T(8,128)}), f32[96,256]{1,0:T(8,128)}) %all-reduce.4.cloned.1.call-update) | async-done | bytes 98320 | tf_op jit(solution)/shard_map/psum | solution.py:123
  418.7 1.6 multiply_subtract_fusion
  (75 shorter events, 6.7 us)
Async XLA Ops:
  7.2 73.8 %all-gather.2.cloned.1.call-start = ((), (), s32[]{:S(2)}) async-start(), calls=%async_computation.1 | async-start | bytes 1622016 | tf_op jit(solution)/shard_map/all_gather | solution.py:54
  8.7 8.4 %copy-start = (bf16[1,2,16,36,256]{4,2,3,1,0:T(8,128)(2,1)S(1)}, bf16[1,2,16,36,256]{4,2,3,1,0:T(8,128)(2,1)}, u32[]{:S(2)}) copy-start(bf16[1,2,16,36,256]{4,2,3,1,0:T(8,128)(2,1)} %param.7) | copy-start | bytes 1769476
  8.8 243.3 %reduce-scatter.2.cloned.1.call-start = ((), (), s32[]{:S(2)}) async-start(), calls=%async_computation.2 | async-start | bytes 3244032 | tf_op jit(solution)/shard_map/reduce_scatter | solution.py:122
  10.9 18.9 %collective-permute-start.3 = (bf16[1,1,16,36,256]{4,3,2,1,0:T(8,128)(2,1)S(1)}, bf16[1,1,16,36,256]{4,3,2,1,0:T(8,128)(2,1)S(1)}, u32[]{:S(2)}, u32[]{:S(2)}) collective-permute-start(bf16[1,1,16,36,256]{4,3,2,1,0:T(8,128)(2,1)S(1)} %get-tuple-element.25), channel_id=1, source_target_pairs={{0,1},{1,2},{2,3},{3,4},{4,5},{5,6},{6,7},{7,8},{8,9},{9,10},{10,1... | collective-permute-start | bytes 884744 | tf_op jit(solution)/shard_map/ppermute | solution.py:22
  15.8 67.1 %collective-permute-start.2 = (bf16[1,1,16,36,256]{4,3,2,1,0:T(8,128)(2,1)}, bf16[1,1,16,36,256]{4,3,2,1,0:T(8,128)(2,1)}, u32[]{:S(2)}, u32[]{:S(2)}) collective-permute-start(bf16[1,1,16,36,256]{4,3,2,1,0:T(8,128)(2,1)} %get-tuple-element.24), channel_id=1, source_target_pairs={{1,0},{2,1},{3,2},{4,3},{5,4},{6,5},{7,6},{8,7},{9,8},{10,9},{11,1... | collective-permute-start | bytes 884744 | tf_op jit(solution)/shard_map/ppermute | solution.py:25
  17.9 64.5 %copy-start.2 = (bf16[1,2,16,36,256]{4,2,3,1,0:T(8,128)(2,1)S(1)}, bf16[1,2,16,36,256]{4,2,3,1,0:T(8,128)(2,1)}, u32[]{:S(2)}) copy-start(bf16[1,2,16,36,256]{4,2,3,1,0:T(8,128)(2,1)} %param.8) | copy-start | bytes 1769476
  29.8 0.7 copy-start.12
  80.9 1.6 copy-start.1
  87.1 0.7 copy-start.15
  87.1 0.7 copy-start.16
  89.0 1.1 copy-start.5
  90.1 1.7 copy-start.3
  106.0 19.3 %collective-permute-start = (bf16[1,1,16,36,256]{4,3,2,1,0:T(8,128)(2,1)S(1)}, bf16[1,1,16,36,256]{4,3,2,1,0:T(8,128)(2,1)S(1)}, u32[]{:S(2)}, u32[]{:S(2)}) collective-permute-start(bf16[1,1,16,36,256]{4,3,2,1,0:T(8,128)(2,1)S(1)} %get-tuple-element.26), channel_id=1, source_target_pairs={{0,1},{1,2},{2,3},{3,4},{4,5},{5,6},{6,7},{7,8},{8,9},{9,10},{10,1... | collective-permute-start | bytes 884744 | tf_op jit(solution)/shard_map/ppermute | solution.py:22
  112.1 13.3 %copy-start.4 = (bf16[1,2,16,36,256]{4,2,3,1,0:T(8,128)(2,1)S(1)}, bf16[1,2,16,36,256]{4,2,3,1,0:T(8,128)(2,1)}, u32[]{:S(2)}) copy-start(bf16[1,2,16,36,256]{4,2,3,1,0:T(8,128)(2,1)} %param.8) | copy-start | bytes 1769476
  112.1 15.6 %collective-permute-start.1 = (bf16[1,1,16,36,256]{4,3,2,1,0:T(8,128)(2,1)S(1)}, bf16[1,1,16,36,256]{4,3,2,1,0:T(8,128)(2,1)S(1)}, u32[]{:S(2)}, u32[]{:S(2)}) collective-permute-start(bf16[1,1,16,36,256]{4,3,2,1,0:T(8,128)(2,1)S(1)} %get-tuple-element.27), channel_id=1, source_target_pairs={{1,0},{2,1},{3,2},{4,3},{5,4},{6,5},{7,6},{8,7},{9,8},{10,9},{11,1... | collective-permute-start | bytes 884744 | tf_op jit(solution)/shard_map/ppermute | solution.py:25
  125.3 1.2 copy-start.8
  127.7 0.7 copy-start.10
  129.7 1.1 copy-start.6
  129.7 289.0 %all-reduce.4.cloned.1.call-start = ((), (), s32[]{:S(2)}) async-start(), calls=%async_computation.3 | async-start | bytes 196608 | tf_op jit(solution)/shard_map/psum | solution.py:123
  131.7 99.9 %copy-start.11 = (bf16[1,1,16,36,256]{4,3,2,1,0:T(8,128)(2,1)S(1)}, bf16[1,1,16,36,256]{4,3,2,1,0:T(8,128)(2,1)}, u32[]{:S(2)}) copy-start(bf16[1,1,16,36,256]{4,3,2,1,0:T(8,128)(2,1)} %copy-done.10) | copy-start | bytes 884740
  231.6 20.5 %copy-start.9 = (bf16[1,1,16,36,256]{4,3,2,1,0:T(8,128)(2,1)S(1)}, bf16[1,1,16,36,256]{4,3,2,1,0:T(8,128)(2,1)}, u32[]{:S(2)}) copy-start(bf16[1,1,16,36,256]{4,3,2,1,0:T(8,128)(2,1)} %copy-done.8) | copy-start | bytes 884740
  254.3 164.3 %copy-start.7 = (f32[96,256]{1,0:T(8,128)S(1)}, f32[96,256]{1,0:T(8,128)}, u32[]{:S(2)}) copy-start(f32[96,256]{1,0:T(8,128)} %param.9) | copy-start | bytes 294916
  254.3 164.3 %copy-start.13 = (f32[96,256]{1,0:T(8,128)S(1)}, f32[96,256]{1,0:T(8,128)}, u32[]{:S(2)}) copy-start(f32[96,256]{1,0:T(8,128)} %param.10) | copy-start | bytes 294916
  254.4 164.3 %copy-start.14 = (f32[96,256]{1,0:T(8,128)S(1)}, f32[96,256]{1,0:T(8,128)}, u32[]{:S(2)}) copy-start(f32[96,256]{1,0:T(8,128)} %param.11) | copy-start | bytes 294916
Sparse Core Ops, SparseCore 0:
  10.7 70.1 all-gather.1
  129.8 122.2 reduce-scatter.1
  255.0 163.6 all-reduce.3
where the time goes:
time: 427 us
  waiting for transfers between devices  255 us (60%)
  blocking collectives  98.4 us (23%)
  matrix products  29.6 us (7%)
  between operations  14.1 us (3%)
  starting transfers between devices  12.7 us (3%)
  local copies, waits for them, and re-layouts  9.06 us (2%)
  other arithmetic  7.8 us (2%)
    psum x1, waiting for transfers between devices, shards(): gradient = lax.psum(row_block, 'tm')  163 us
    psum x1, blocking collectives, shards(): norm_grads = lax.psum(jnp.stack([gain_grad, bias_grad]), ('blk', 'tm'))  98.4 us
    all_gather x1, waiting for transfers between devices, shards(): lax.all_gather(conv_master.astype(jnp.bfloat16), 'blk', axis=0, tiled=True)  50.4 us
    ppermute x2, waiting for transfers between devices, extended(): lax.ppermute(lax.slice_in_dim(block, block.shape[dim] - width, None, axis...  22.2 us
    reduce_scatter x1, waiting for transfers between devices, shards(): lax.psum_scatter(local_gradient, 'blk', scatter_dimension=0, tiled=True)  19.1 us
    ppermute x2, starting transfers between devices, extended(): lax.ppermute(lax.slice_in_dim(block, block.shape[dim] - width, None, axis...  9.9 us
    dot_general x9, matrix products, shards(): jnp.einsum('bfhwc,bfhwd->cd', window, space_grad, preferred_element_type=...  9.86 us
  transfers between devices with their start and end apart: 7, of which 5 were waited for; matrix products, arithmetic and copies ran while one was open for 4% of the time, Pallas kernels for 0%

commit v1 on v0

--- a/solution.py
+++ b/solution.py
@@ -1,6 +1,8 @@
 import jax
 import jax.numpy as jnp
 from jax import lax
+from jax.experimental import pallas as pl
+from jax.experimental.pallas import tpu as pltpu
 from jax.sharding import PartitionSpec as P
 
 GROUPS = 32
@@ -42,6 +44,336 @@
     update = new_first / bias_first / (jnp.sqrt(new_second / bias_second) + adam_eps)
     return (master - learn_rate * update, new_first, new_second)
 
+MESH = pl.DeviceIdType.MESH
+VMEM = pl.BlockSpec(memory_space=pltpu.VMEM)
+
+
+def place():
+    me = lax.axis_index("blk")
+    return me // 16, lax.rem(me // 2, 8), lax.rem(me, 2), lax.axis_index("tm")
+
+
+def owner(x, y, c):
+    return x * 16 + lax.rem(y + 8, 8) * 2 + c
+
+
+def greet(peers):
+    barrier = pltpu.get_barrier_semaphore()
+    for peer in peers:
+        pl.semaphore_signal(barrier, inc=1, device_id=peer, device_id_type=MESH)
+    pl.semaphore_wait(barrier, len(peers))
+
+
+def send(src, dst, send_sem, recv_sem, peer):
+    copy = pltpu.make_async_remote_copy(
+        src_ref=src,
+        dst_ref=dst,
+        send_sem=send_sem,
+        recv_sem=recv_sem,
+        device_id=peer,
+        device_id_type=MESH,
+    )
+    copy.start()
+    return copy
+
+
+def gather_kernel(w_ref, out_ref, ring_send, ring_recv, pair_send, pair_recv, x_send, x_recv):
+    x, y, c, t = place()
+    partner = (owner(x, y, 1 - c), t)
+    across = (owner(1 - x, y, c), t)
+    ring = ((owner(x, y + 1, c), t), (owner(x, y - 1, c), t))
+    greet([partner, across, ring[0], ring[1]])
+    started = []
+
+    def pass_on(src, k, offset):
+        slot = k * 8 + offset % 8
+        dst = out_ref.at[owner(x if k == 0 else 1 - x, y + offset, c)]
+        started.append(send(src, dst, pair_send.at[slot], pair_recv.at[slot], partner))
+
+    def hop(src, d, s, k):
+        offset = -s if d == 0 else s
+        dst = out_ref.at[owner(x if k == 0 else 1 - x, y + offset, c)]
+        copy = send(src, dst, ring_send.at[d, s, k], ring_recv.at[d, s, k], ring[d])
+        started.append(copy)
+        return copy
+
+    mine = owner(x, y, c)
+    x_copy = send(w_ref, out_ref.at[mine], x_send, x_recv, across)
+    copies = {}
+    for d in range(2):
+        copies[d, 0] = hop(w_ref, d, 0, 0)
+    pass_on(w_ref, 0, 0)
+    out_ref[mine] = w_ref[...]
+    x_copy.wait_recv()
+    other = out_ref.at[owner(1 - x, y, c)]
+    for d in range(2):
+        copies[d, 1] = hop(other, d, 0, 1)
+    pass_on(other, 1, 0)
+    for s in range(1, 5):
+        for k in range(2):
+            for d in range(2):
+                if s == 4 and k != d:
+                    continue
+                offset = -s if d == 0 else s
+                copies[d, k].wait_recv()
+                block = out_ref.at[owner(x if k == 0 else 1 - x, y + offset, c)]
+                if s < 3 or (s == 3 and k == d):
+                    copies[d, k] = hop(block, d, s, k)
+                pass_on(block, k, offset)
+    x_copy.wait_send()
+    for copy in started:
+        copy.wait_send()
+    for slot in range(16):
+        k, offset = slot // 8, slot % 8
+        block = out_ref.at[owner(x if k == 0 else 1 - x, y + offset, 1 - c)]
+        pltpu.make_async_remote_copy(
+            src_ref=w_ref,
+            dst_ref=block,
+            send_sem=pair_send.at[slot],
+            recv_sem=pair_recv.at[slot],
+            device_id=partner,
+            device_id_type=MESH,
+        ).wait_recv()
+
+
+def gather_weights(rows):
+    dma = pltpu.SemaphoreType.DMA
+    return pl.pallas_call(
+        gather_kernel,
+        out_shape=jax.ShapeDtypeStruct((32,) + rows.shape, rows.dtype),
+        in_specs=[VMEM],
+        out_specs=VMEM,
+        scratch_shapes=[dma((2, 4, 2)), dma((2, 4, 2)), dma((16,)), dma((16,)), dma(()), dma(())],
+        compiler_params=pltpu.CompilerParams(collective_id=0, has_side_effects=True),
+        name="gather_weights",
+    )(rows)
+
+
+PAIR_ORDER = (4, 3, -3, 2, -2, 1, -1, 0)
+
+
+def reduce_kernel(
+    g_ref,
+    n_ref,
+    out_ref,
+    norm_ref,
+    pair_buf,
+    ring_src,
+    ring_dst,
+    x_src,
+    x_dst,
+    held,
+    z_dst,
+    h_src,
+    h_dst,
+    z_src,
+    n_pair,
+    n_y_src,
+    n_y,
+    n_x_src,
+    n_x,
+    n_z_src,
+    n_z,
+    n_h_src,
+    n_h,
+    pair_s,
+    pair_r,
+    ring_s,
+    ring_r,
+    zs_s,
+    zs_r,
+    zg_s,
+    zg_r,
+    one_s,
+    one_r,
+    ny_s,
+    ny_r,
+    nz_s,
+    nz_r,
+):
+    f32 = jnp.float32
+    x, y, c, t = place()
+    z, h = t // 2, lax.rem(t, 2)
+    mine = owner(x, y, c)
+    partner = (owner(x, y, 1 - c), t)
+    across = (owner(1 - x, y, c), t)
+    far = (mine, z * 2 + 1 - h)
+    y_peers = [(owner(x, y + i, c), t) for i in range(1, 8)]
+    z_peers = [(mine, lax.rem(z + i, 8) * 2 + h) for i in range(1, 8)]
+    ring = (y_peers[0], y_peers[6])
+    greet([partner, across, far] + y_peers + z_peers)
+    started = []
+
+    def go(*args):
+        copy = send(*args)
+        started.append(copy)
+        return copy
+
+    norm_pair = go(n_ref, n_pair, one_s.at[0], one_r.at[0], partner)
+    pair = []
+    for m, offset in enumerate(PAIR_ORDER):
+        target = lax.rem(y + offset + 8, 8)
+        pair.append(
+            go(g_ref.at[:, target, 1 - c], pair_buf.at[m], pair_s.at[m], pair_r.at[m], partner)
+        )
+    arrived = {}
+    waited = set()
+
+    def local(offset, k):
+        m = PAIR_ORDER.index(offset)
+        if m not in waited:
+            pair[m].wait_recv()
+            waited.add(m)
+        return g_ref[k, lax.rem(y + offset + 8, 8), c] + pair_buf[m, k]
+
+    for s in range(4):
+        for k in range(2):
+            for d in range(2):
+                if s == 0 and k != d:
+                    continue
+                offset = 4 if s == 0 else (4 - s if d == 0 else s - 4)
+                value = local(offset, k)
+                if (d, k) in arrived:
+                    arrived[d, k].wait_recv()
+                    value = value + ring_dst[d, s - 1, k].astype(f32)
+                ring_src[d, s, k] = value.astype(ring_src.dtype)
+                arrived[d, k] = go(
+                    ring_src.at[d, s, k],
+                    ring_dst.at[d, s, k],
+                    ring_s.at[d, s, k],
+                    ring_r.at[d, s, k],
+                    ring[d],
+                )
+        if s == 0:
+            norm_pair.wait_recv()
+            part = n_ref[...] + n_pair[...]
+            n_y_src[...] = part
+            n_y[y] = part
+            norm_y = [
+                go(n_y_src, n_y.at[y], ny_s.at[i], ny_r.at[i], peer)
+                for i, peer in enumerate(y_peers)
+            ]
+        if s == 1:
+            for copy in norm_y:
+                copy.wait_recv()
+            part = n_y[0]
+            for i in range(1, 8):
+                part = part + n_y[i]
+            n_x_src[...] = part
+            norm_x = go(n_x_src, n_x, one_s.at[1], one_r.at[1], across)
+        if s == 2:
+            norm_x.wait_recv()
+            part = n_x_src[...] + n_x[...]
+            n_z_src[...] = part
+            n_z[z] = part
+            norm_z = [
+                go(n_z_src, n_z.at[z], nz_s.at[i], nz_r.at[i], peer)
+                for i, peer in enumerate(z_peers)
+            ]
+        if s == 3:
+            for copy in norm_z:
+                copy.wait_recv()
+            part = n_z[0]
+            for i in range(1, 8):
+                part = part + n_z[i]
+            n_h_src[...] = part
+            norm_h = go(n_h_src, n_h, one_s.at[2], one_r.at[2], far)
+
+    totals = []
+    for k in range(2):
+        value = local(0, k)
+        for d in range(2):
+            arrived[d, k].wait_recv()
+            value = value + ring_dst[d, 3, k].astype(f32)
+        totals.append(value)
+    keep = jnp.where(x == 0, totals[0], totals[1])
+    x_src[...] = jnp.where(x == 0, totals[1], totals[0])
+    x_copy = go(x_src, x_dst, one_s.at[3], one_r.at[3], across)
+    x_copy.wait_recv()
+    value = keep + x_dst[...]
+    for p in range(8):
+        held[p] = value[(p // 2) * 24 : (p // 2) * 24 + 24, (p % 2) * 128 : (p % 2) * 128 + 128]
+    scatter = [
+        go(held.at[lax.rem(z + i + 1, 8)], z_dst.at[z], zs_s.at[i], zs_r.at[i], peer)
+        for i, peer in enumerate(z_peers)
+    ]
+    z_dst[z] = held[z]
+    for copy in scatter:
+        copy.wait_recv()
+    part = z_dst[0]
+    for i in range(1, 8):
+        part = part + z_dst[i]
+    h_src[...] = part
+    h_copy = go(h_src, h_dst, one_s.at[4], one_r.at[4], far)
+    norm_h.wait_recv()
+    norm_ref[...] = n_h_src[...] + n_h[...]
+    h_copy.wait_recv()
+    part = h_src[...] + h_dst[...]
+    z_src[...] = part
+    out_ref[z] = part
+    spread = [
+        go(z_src, out_ref.at[z], zg_s.at[i], zg_r.at[i], peer) for i, peer in enumerate(z_peers)
+    ]
+    for copy in spread:
+        copy.wait_recv()
+    for copy in started:
+        copy.wait_send()
+
+
+def reduce_gradient(gradient, norms):
+    f32, bf16 = jnp.float32, jnp.bfloat16
+    dma, vmem = pltpu.SemaphoreType.DMA, pltpu.VMEM
+    small = vmem((8, 128), f32)
+    eight = vmem((8, 8, 128), f32)
+    return pl.pallas_call(
+        reduce_kernel,
+        out_shape=(
+            jax.ShapeDtypeStruct((8, 24, 128), f32),
+            jax.ShapeDtypeStruct((8, 128), f32),
+        ),
+        in_specs=[VMEM, VMEM],
+        out_specs=(VMEM, VMEM),
+        scratch_shapes=[
+            vmem((8, 2, 96, 256), f32),
+            vmem((2, 4, 2, 96, 256), bf16),
+            vmem((2, 4, 2, 96, 256), bf16),
+            vmem((96, 256), f32),
+            vmem((96, 256), f32),
+            vmem((8, 24, 128), f32),
+            vmem((8, 24, 128), f32),
+            vmem((24, 128), f32),
+            vmem((24, 128), f32),
+            vmem((24, 128), f32),
+            small,
+            small,
+            eight,
+            small,
+            small,
+            small,
+            eight,
+            small,
+            small,
+            dma((8,)),
+            dma((8,)),
+            dma((2, 4, 2)),
+            dma((2, 4, 2)),
+            dma((7,)),
+            dma((7,)),
+            dma((7,)),
+            dma((7,)),
+            dma((5,)),
+            dma((5,)),
+            dma((7,)),
+            dma((7,)),
+            dma((7,)),
+            dma((7,)),
+        ],
+        compiler_params=pltpu.CompilerParams(
+            collective_id=1, has_side_effects=True, vmem_limit_bytes=40 * 2**20
+        ),
+        name="reduce_gradient",
+    )(gradient.reshape(2, 8, 2, 96, 256), norms)
+
 
 def shards(clips, cotangent, conv_master, first_moment, second_moment, norm_gain, norm_bias):
     f32 = jnp.float32
@@ -51,7 +383,7 @@
         clips.shape[3],
         clips.shape[4],
     )
-    weights = lax.all_gather(conv_master.astype(jnp.bfloat16), "blk", axis=0, tiled=True)
+    weights = gather_weights(conv_master.astype(jnp.bfloat16)).reshape(12 * channels, channels)
     inputs32 = clips.astype(f32)
     act32, pullback = jax.vjp(norm_act, inputs32, norm_gain, norm_bias)
     act = act32.astype(jnp.bfloat16)
@@ -77,7 +409,7 @@
             preferred_element_type=f32,
         )
     block_out = (inputs32 + temporal).astype(jnp.bfloat16)
-    back_weights = lax.all_gather(conv_master.astype(jnp.bfloat16), "blk", axis=0, tiled=True)
+    back_weights = weights
     grad_padded = extended(cotangent, (("tm", 1),), 1)
     space_grad32 = jnp.zeros(clips.shape, f32)
     temporal_grads = []
@@ -92,8 +424,8 @@
         temporal_grads.append(
             jnp.einsum(
                 "bfhwc,bfhwd->cd",
-                space_padded[:, frame_tap : frame_tap + frames],
-                cotangent,
+                space,
+                grad_padded[:, 2 - frame_tap : 2 - frame_tap + frames],
                 preferred_element_type=f32,
             )
         )
@@ -118,9 +450,10 @@
     input_term, gain_grad, bias_grad = pullback(act_grad)
     input_grad = (cotangent.astype(f32) + input_term).astype(jnp.bfloat16)
     local_gradient = jnp.concatenate(spatial_grads + temporal_grads, axis=0)
-    norm_grads = lax.psum(jnp.stack([gain_grad, bias_grad]), ("blk", "tm"))
-    row_block = lax.psum_scatter(local_gradient, "blk", scatter_dimension=0, tiled=True)
-    gradient = lax.psum(row_block, "tm")
+    norms = jnp.pad(jnp.concatenate([gain_grad, bias_grad]).reshape(4, 128), ((0, 4), (0, 0)))
+    pieces, norm_sums = reduce_gradient(local_gradient, norms)
+    norm_grads = norm_sums[:4].reshape(2, channels)
+    gradient = pieces.reshape(4, 2, 24, 128).transpose(0, 2, 1, 3).reshape(96, channels)
     new_master, new_first, new_second = adam_update(
         gradient, conv_master, first_moment, second_moment
     )

time: 427 us -> 135 us (0.32)
  the two profiles are of different devices: /device:TPU:8 before, /device:TPU:18 now
where the time goes in v1:
time: 135 us
  Pallas kernels  79.8 us (59%)
  matrix products  25 us (19%)
  starting transfers between devices  14.4 us (11%)
  local copies, waits for them, and re-layouts  7.71 us (6%)
  other arithmetic  6.53 us (5%)
    pallas_call x1, Pallas kernels, reduce_gradient(): pl.pallas_call(reduce_kernel, out_shape=(jax.ShapeDtypeStruct((8, 24, 128...  47.5 us
    pallas_call x1, Pallas kernels, gather_weights(): pl.pallas_call(gather_kernel, out_shape=jax.ShapeDtypeStruct((32,) + rows...  32.3 us
    ppermute x2, starting transfers between devices, extended(): lax.ppermute(lax.slice_in_dim(block, block.shape[dim] - width, None, axis...  11.7 us
    dot_general x9, matrix products, shards(): jnp.einsum('bfhwd,cd->bfhwc', back_window, tap, preferred_element_type=f32)  5.37 us
    dot_general x3, matrix products, shards(): jnp.einsum('bfhwd,cd->bfhwc', grad_padded[:, 2 - frame_tap:2 - frame_tap...  5.29 us
    dot_general x3, matrix products, shards(): jnp.einsum('bfhwc,cd->bfhwd', space_padded[:, frame_tap:frame_tap + frame...  4.39 us
    unnamed x33, local copies, waits for them, and re-layouts  4.19 us
    dot_general x9, matrix products, shards(): jnp.einsum('bfhwc,bfhwd->cd', window, space_grad, preferred_element_type=...  3.49 us
  transfers between devices with their start and end apart: 4, of which 0 were waited for; matrix products, arithmetic and copies ran while one was open for 12% of the time, Pallas kernels for 59%

profile of v1, /device:TPU:18, one launch (start us, length us, event | category | flops | bytes accessed | tf_op | source)
XLA Modules:
  0.0 134.7 jit_solution(12736985029600653941)
XLA Ops:
  0.6 1.3 copy.25
  2.0 0.9 fusion.179
  2.8 4.9 %collective-permute-start.3 = (bf16[1,1,16,36,256]{4,3,2,1,0:T(8,128)(2,1)}, bf16[1,1,16,36,256]{4,3,2,1,0:T(8,128)(2,1)}, u32[]{:S(2)}, u32[]{:S(2)}) collective-permute-start(bf16[1,1,16,36,256]{4,3,2,1,0:T(8,128)(2,1)} %get-tuple-element.29), channel_id=1, source_target_pairs={{0,1},{1,2},{2,3},{3,4},{4,5},{5,6},{6,7},{7,8},{8,9},{9,10},{10,1... | collective-permute-start | bytes 884744 | tf_op jit(solution)/shard_map/ppermute | solution.py:24
  7.7 1.3 collective-permute-start.2
  9.0 0.6 convert_element_type.39.w_ref
  9.7 32.3 %gather_weights.1 = bf16[32,96,256]{2,1,0:T(8,128)(2,1)} custom-call(bf16[96,256]{1,0:T(8,128)(2,1)} %convert_element_type.39.w_ref), custom_call_target="tpu_custom_call" | custom-call | tf_op jit(solution)/shard_map/gather_weights/pallas_call | solution.py:141
  42.5 2.5 %fusion.96 = f32[2,16,36,256]{3,2,1,0:T(8,128)} fusion(bf16[2,16,36,256]{3,1,2,0:T(8,128)(2,1)S(1)} %bitcast.339, bf16[3072,256]{1,0:T(8,128)(2,1)} %bitcast.315), kind=kOutput, calls=%fused_computation.134 | convolution fusion | flops 150994944 | bytes 1900544 | tf_op jit(solution)/shard_map/bfhwd,cd->bfhwc/dot_general | solution.py:418
  45.7 1.4 %fusion.125 = f32[2,16,36,256]{3,2,1,0:T(8,128)S(1)} fusion(bf16[1,2,16,36,256]{4,3,2,1,0:T(8,128)(2,1)S(1)} %copy.25, bf16[1,1,16,36,256]{4,3,2,1,0:T(8,128)(2,1)} %collective-permute-done.3, bf16[3072,256]{1,0:T(8,128)(2,1)S(1)} %bitcast.316), kind=kOutput, calls=%fused_computation.160 | convolution fusion | flops 151289856 | bytes 2260992 | tf_op jit(solution)/shard_map/bfhwd,cd->bfhwc/dot_general | solution.py:418
  47.2 1.4 %fusion.9 = bf16[2,16,36,256]{3,2,1,0:T(8,128)(2,1)S(1)} fusion(f32[2,16,36,256]{3,2,1,0:T(8,128)S(1)} %fusion.125, f32[2,16,36,256]{3,2,1,0:T(8,128)S(1)} %copy-done.7, bf16[1,1,16,36,256]{4,3,2,1,0:T(8,128)(2,1)} %collective-permute-done.2, bf16[1,2,16,36,256]{4,3,2,1,0:T(8,128)(2,1)S(1)} %copy.25, bf16[3072,256]{1,0:T(8,128)(2,1)S(1)} %bitcast.317), kind=kOutput, calls=%fused_computation.32 | convolution fusion | flops 152174592 | bytes 4292608 | tf_op jit(solution)/shard_map/bfhwd,cd->bfhwc/dot_general | solution.py:418
  48.5 0.4 fusion.66
  48.9 0.4 convolution_add_fusion.7
  49.3 0.4 convolution_add_fusion.6
  49.7 0.4 convolution_add_fusion.5
  50.5 0.4 convolution_add_fusion.3
  50.9 0.4 convolution_add_fusion.2
  51.3 0.4 convolution_add_fusion.1
  52.0 2.3 %fusion.26 = (f32[2,256]{1,0:T(2,128)S(1)}, f32[2,16,36,256]{3,2,1,0:T(8,128)}) fusion(f32[256]{0:T(256)S(1)} %copy-done.13, f32[2,256]{1,0:T(2,128)S(1)} %sub.42, bf16[1,2,16,36,256]{4,2,3,1,0:T(8,128)(2,1)S(1)} %copy-done, f32[256]{0:T(256)S(1)} %copy-done.14, f32[2,256]{1,0:T(2,128)S(1)} %mul.163, f32[2,16,36,256]{3,2,1,0:T(8,128)S(1)} %convolution_add_fusion.1, ...), kind=kOutput, calls=%fused_computation.49 | convolution fusion | flops 156597760 | bytes 3876864 | tf_op jit(solution)/shard_map/bfhwd,cd->bfhwc/dot_general | solution.py:447
  55.1 1.8 %fusion.37 = (f32[256]{0:T(256)S(1)}, f32[2,256]{1,0:T(2,128)S(1)}, f32[256]{0:T(256)S(1)}) fusion(f32[2,16,36,256]{3,2,1,0:T(8,128)} %get-tuple-element.35, f32[2,256]{1,0:T(2,128)S(1)} %mul.163, f32[2,256]{1,0:T(2,128)S(1)} %sub.42, bf16[1,2,16,36,256]{4,2,3,1,0:T(8,128)(2,1)S(1)} %copy-done, f32[256]{0:T(256)S(1)} %copy-done.13), kind=kLoop, calls=%fused_computation.60 | loop fusion | flops 2653184 | bytes 1778688 | tf_op jit(solution)/shard_map/transpose(jvp())/reduce_sum | solution.py:38
  57.3 2.2 %fusion.14 = (bf16[1,2,16,36,256]{4,3,2,1,0:T(8,128)(2,1)S(1)}, bf16[1,2,16,36,256]{4,3,2,1,0:T(8,128)(2,1)S(1)}) fusion(f32[2,16,36,256]{3,2,1,0:T(8,128)} %get-tuple-element.35, f32[2,256]{1,0:T(2,128)S(1)} %broadcast_in_dim.7, f32[2,256]{1,0:T(2,128)S(1)} %mul.188, f32[256]{0:T(256)S(1)} %copy-done.13, f32[2,256]{1,0:T(2,128)S(1)} %mul.163, ...), kind=kLoop, calls=%fused_computation.37 | loop fusion | flops 5308416 | bytes 3549184 | tf_op jit(solution)/shard_map/convert_element_type | solution.py:451
  59.5 0.4 fusion.85
  59.8 0.4 fusion.49
  61.0 0.4 convolution_add_fusion.15
  61.7 0.4 convolution_add_fusion.13
  62.0 0.4 convolution_add_fusion.12
  62.8 0.4 fusion.10
  63.2 1.4 %fusion.127 = f32[2,16,36,256]{3,2,1,0:T(8,128)} fusion(bf16[2,16,36,256]{3,2,1,0:T(8,128)(2,1)S(1)} %fusion.10, bf16[3072,256]{1,0:T(8,128)(2,1)S(1)} %bitcast.336), kind=kOutput, calls=%fused_computation.174 | convolution fusion | flops 150994944 | bytes 1966080 | tf_op jit(solution)/shard_map/bfhwc,cd->bfhwd/dot_general | solution.py:405
  64.6 0.9 fusion.180
  65.4 1.5 %collective-permute-start.1 = (bf16[1,1,16,36,256]{4,3,2,1,0:T(8,128)(2,1)}, bf16[1,1,16,36,256]{4,3,2,1,0:T(8,128)(2,1)}, u32[]{:S(2)}, u32[]{:S(2)}) collective-permute-start(bf16[1,1,16,36,256]{4,3,2,1,0:T(8,128)(2,1)} %get-tuple-element.31), channel_id=1, source_target_pairs={{1,0},{2,1},{3,2},{4,3},{5,4},{6,5},{7,6},{8,7},{9,8},{10,9},{11,1... | collective-permute-start | bytes 884744 | tf_op jit(solution)/shard_map/ppermute | solution.py:27
  66.9 6.8 %collective-permute-start = (bf16[1,1,16,36,256]{4,3,2,1,0:T(8,128)(2,1)}, bf16[1,1,16,36,256]{4,3,2,1,0:T(8,128)(2,1)}, u32[]{:S(2)}, u32[]{:S(2)}) collective-permute-start(bf16[1,1,16,36,256]{4,3,2,1,0:T(8,128)(2,1)} %get-tuple-element.30), channel_id=1, source_target_pairs={{0,1},{1,2},{2,3},{3,4},{4,5},{5,6},{6,7},{7,8},{8,9},{9,10},{10,1... | collective-permute-start | bytes 884744 | tf_op jit(solution)/shard_map/ppermute | solution.py:24
  73.7 0.4 fusion.48
  74.1 0.4 fusion.47
  74.5 0.4 fusion.46
  74.9 0.4 fusion.45
  75.3 0.4 fusion.44
  75.7 0.4 fusion.43
  76.1 0.4 fusion.42
  76.5 0.4 fusion.41
  76.9 0.7 copy-done.3
  77.6 1.4 %fusion.40 = f32[3072,256]{1,0:T(8,128)S(1)} fusion(f32[3072,256]{1,0:T(8,128)S(1)} %fusion.41, bf16[2,16,36,256]{3,2,1,0:T(8,128)(2,1)S(1)} %fusion.10, bf16[1,1,16,36,256]{4,3,2,1,0:T(8,128)(2,1)} %collective-permute-done.2, bf16[1,2,16,36,256]{4,3,2,1,0:T(8,128)(2,1)S(1)} %copy-done.3), kind=kOutput, calls=%fused_computation.67 | convolution fusion | flops 151289856 | bytes 1867776 | tf_op jit(solution)/shard_map/bfhwc,bfhwd->cd/dot_general | solution.py:425
  79.0 0.4 fusion.39
  79.5 1.4 %fusion.38 = f32[3072,256]{1,0:T(8,128)S(1)} fusion(f32[3072,256]{1,0:T(8,128)S(1)} %fusion.39, bf16[2,16,36,256]{3,2,1,0:T(8,128)(2,1)S(1)} %fusion.10, bf16[1,2,16,36,256]{4,3,2,1,0:T(8,128)(2,1)S(1)} %copy-done.3, bf16[1,1,16,36,256]{4,3,2,1,0:T(8,128)(2,1)} %collective-permute-done.3), kind=kOutput, calls=%fused_computation.63 | convolution fusion | flops 151289856 | bytes 1867776 | tf_op jit(solution)/shard_map/bfhwc,bfhwd->cd/dot_general | solution.py:425
  80.9 47.5 %reduce_gradient.1 = (f32[8,24,128]{2,1,0:T(8,128)S(1)}, f32[8,128]{1,0:T(8,128)S(1)}) custom-call(f32[2,8,2,96,256]{4,3,2,1,0:T(8,128)S(1)} %bitcast.302, f32[8,128]{1,0:T(8,128)S(1)} %select_maximum_fusion.n_ref), custom_call_target="tpu_custom_call" | custom-call | tf_op jit(solution)/shard_map/reduce_gradient/pallas_call | solution.py:328
  128.5 0.7 multiply_subtract_fusion
  129.2 0.9 copy.34
  130.2 0.6 reshape.361
  130.8 1.4 %fusion.53 = f32[2,16,36,256]{3,2,1,0:T(8,128)S(1)} fusion(bf16[1,1,16,36,256]{4,3,2,1,0:T(8,128)(2,1)} %collective-permute-done.1, bf16[1,2,16,36,256]{4,3,2,1,0:T(8,128)(2,1)S(1)} %bitcast.313, bf16[3072,256]{1,0:T(8,128)(2,1)S(1)} %bitcast.337), kind=kOutput, calls=%fused_computation.92 | convolution fusion | flops 151289856 | bytes 2260992 | tf_op jit(solution)/shard_map/bfhwc,cd->bfhwd/dot_general | solution.py:405
  132.2 1.6 %fusion.11 = bf16[1,2,16,36,256]{4,3,2,1,0:T(8,128)(2,1)S(1)} fusion(f32[2,16,36,256]{3,2,1,0:T(8,128)S(1)} %fusion.53, f32[2,16,36,256]{3,2,1,0:T(8,128)S(1)} %copy-done.8, bf16[1,2,16,36,256]{4,3,2,1,0:T(8,128)(2,1)S(1)} %bitcast.314, bf16[1,1,16,36,256]{4,3,2,1,0:T(8,128)(2,1)} %collective-permute-done, bf16[1,2,16,36,256]{4,2,3,1,0:T(8,128)(2,1)S(1)} %copy-done, ...), kind=kOutput, calls=%fused_computation.34 | convolution fusion | flops 152764416 | bytes 4882432 | tf_op jit(solution)/shard_map/bfhwc,cd->bfhwd/dot_general | solution.py:405
  133.8 0.9 copy.33
  (66 shorter events, 4.5 us)
Async XLA Ops:
  0.6 8.4 %copy-start.9 = (f32[96,256]{1,0:T(8,128)S(1)}, f32[96,256]{1,0:T(8,128)}, u32[]{:S(2)}) copy-start(f32[96,256]{1,0:T(8,128)} %param.9) | copy-start | bytes 294916
  1.9 45.2 %copy-start.2 = (bf16[1,2,16,36,256]{4,3,2,1,0:T(8,128)(2,1)}, bf16[1,2,16,36,256]{4,3,2,1,0:T(8,128)(2,1)S(1)}, u32[]{:S(2)}) copy-start(bf16[1,2,16,36,256]{4,3,2,1,0:T(8,128)(2,1)S(1)} %copy.25) | copy-start | bytes 1769476
  1.9 40.0 %copy-start = (bf16[1,2,16,36,256]{4,2,3,1,0:T(8,128)(2,1)S(1)}, bf16[1,2,16,36,256]{4,2,3,1,0:T(8,128)(2,1)}, u32[]{:S(2)}) copy-start(bf16[1,2,16,36,256]{4,2,3,1,0:T(8,128)(2,1)} %param.7) | copy-start | bytes 1769476
  2.8 39.7 %copy-start.4 = (bf16[1,2,16,36,256]{4,2,3,1,0:T(8,128)(2,1)S(1)}, bf16[1,2,16,36,256]{4,2,3,1,0:T(8,128)(2,1)}, u32[]{:S(2)}) copy-start(bf16[1,2,16,36,256]{4,2,3,1,0:T(8,128)(2,1)} %param.8) | copy-start | bytes 1769476
  2.8 42.8 %collective-permute-start.3 = (bf16[1,1,16,36,256]{4,3,2,1,0:T(8,128)(2,1)}, bf16[1,1,16,36,256]{4,3,2,1,0:T(8,128)(2,1)}, u32[]{:S(2)}, u32[]{:S(2)}) collective-permute-start(bf16[1,1,16,36,256]{4,3,2,1,0:T(8,128)(2,1)} %get-tuple-element.29), channel_id=1, source_target_pairs={{0,1},{1,2},{2,3},{3,4},{4,5},{5,6},{6,7},{7,8},{8,9},{9,10},{10,1... | collective-permute-start | bytes 884744 | tf_op jit(solution)/shard_map/ppermute | solution.py:24
  7.7 39.4 %collective-permute-start.2 = (bf16[1,1,16,36,256]{4,3,2,1,0:T(8,128)(2,1)}, bf16[1,1,16,36,256]{4,3,2,1,0:T(8,128)(2,1)}, u32[]{:S(2)}, u32[]{:S(2)}) collective-permute-start(bf16[1,1,16,36,256]{4,3,2,1,0:T(8,128)(2,1)} %get-tuple-element.28), channel_id=1, source_target_pairs={{1,0},{2,1},{3,2},{4,3},{5,4},{6,5},{7,6},{8,7},{9,8},{10,9},{11,1... | collective-permute-start | bytes 884744 | tf_op jit(solution)/shard_map/ppermute | solution.py:27
  42.5 3.2 %copy-start.1 = (bf16[32,96,256]{2,1,0:T(8,128)(2,1)S(1)}, bf16[32,96,256]{2,1,0:T(8,128)(2,1)}, u32[]{:S(2)}) copy-start(bf16[32,96,256]{2,1,0:T(8,128)(2,1)} %gather_weights.1) | copy-start | bytes 4718596
  45.7 1.5 %copy-start.7 = (f32[2,16,36,256]{3,2,1,0:T(8,128)S(1)}, f32[2,16,36,256]{3,2,1,0:T(8,128)}, u32[]{:S(2)}) copy-start(f32[2,16,36,256]{3,2,1,0:T(8,128)} %fusion.96) | copy-start | bytes 3538948
  51.3 0.7 copy-start.13
  51.3 0.7 copy-start.14
  54.6 2.6 %copy-start.5 = (bf16[1,2,16,36,256]{4,2,3,1,0:T(8,128)(2,1)S(1)}, bf16[1,2,16,36,256]{4,2,3,1,0:T(8,128)(2,1)}, u32[]{:S(2)}) copy-start(bf16[1,2,16,36,256]{4,2,3,1,0:T(8,128)(2,1)} %param.8) | copy-start | bytes 1769476
  65.4 65.3 %collective-permute-start.1 = (bf16[1,1,16,36,256]{4,3,2,1,0:T(8,128)(2,1)}, bf16[1,1,16,36,256]{4,3,2,1,0:T(8,128)(2,1)}, u32[]{:S(2)}, u32[]{:S(2)}) collective-permute-start(bf16[1,1,16,36,256]{4,3,2,1,0:T(8,128)(2,1)} %get-tuple-element.31), channel_id=1, source_target_pairs={{1,0},{2,1},{3,2},{4,3},{5,4},{6,5},{7,6},{8,7},{9,8},{10,9},{11,1... | collective-permute-start | bytes 884744 | tf_op jit(solution)/shard_map/ppermute | solution.py:27
  66.9 65.3 %collective-permute-start = (bf16[1,1,16,36,256]{4,3,2,1,0:T(8,128)(2,1)}, bf16[1,1,16,36,256]{4,3,2,1,0:T(8,128)(2,1)}, u32[]{:S(2)}, u32[]{:S(2)}) collective-permute-start(bf16[1,1,16,36,256]{4,3,2,1,0:T(8,128)(2,1)} %get-tuple-element.30), channel_id=1, source_target_pairs={{0,1},{1,2},{2,3},{3,4},{4,5},{5,6},{6,7},{7,8},{8,9},{9,10},{10,1... | collective-permute-start | bytes 884744 | tf_op jit(solution)/shard_map/ppermute | solution.py:24
  76.5 1.1 copy-start.3
  77.6 1.4 %copy-start.6 = (bf16[1,2,16,36,256]{4,2,3,1,0:T(8,128)(2,1)S(1)}, bf16[1,2,16,36,256]{4,2,3,1,0:T(8,128)(2,1)}, u32[]{:S(2)}) copy-start(bf16[1,2,16,36,256]{4,2,3,1,0:T(8,128)(2,1)} %param.8) | copy-start | bytes 1769476
  80.8 47.6 %copy-start.10 = (f32[96,256]{1,0:T(8,128)S(1)}, f32[96,256]{1,0:T(8,128)}, u32[]{:S(2)}) copy-start(f32[96,256]{1,0:T(8,128)} %param.9) | copy-start | bytes 294916
  80.9 47.6 %copy-start.11 = (f32[96,256]{1,0:T(8,128)S(1)}, f32[96,256]{1,0:T(8,128)}, u32[]{:S(2)}) copy-start(f32[96,256]{1,0:T(8,128)} %param.10) | copy-start | bytes 294916
  80.9 47.6 %copy-start.12 = (f32[96,256]{1,0:T(8,128)S(1)}, f32[96,256]{1,0:T(8,128)}, u32[]{:S(2)}) copy-start(f32[96,256]{1,0:T(8,128)} %param.11) | copy-start | bytes 294916
  130.8 1.5 %copy-start.8 = (f32[2,16,36,256]{3,2,1,0:T(8,128)S(1)}, f32[2,16,36,256]{3,2,1,0:T(8,128)}, u32[]{:S(2)}) copy-start(f32[2,16,36,256]{3,2,1,0:T(8,128)} %fusion.127) | copy-start | bytes 3538948

commit v2 on v1

--- a/solution.py
+++ b/solution.py
@@ -5,8 +5,6 @@
 from jax.experimental.pallas import tpu as pltpu
 from jax.sharding import PartitionSpec as P
 
-GROUPS = 32
-
 
 beta_one = 0.9
 beta_two = 0.999
@@ -14,28 +12,6 @@
 adam_eps = 1e-08
 bias_first = 1.0 - 0.9**10
 bias_second = 1.0 - 0.999**10
-
-
-def extended(block, sides, width):
-    for axis, dim in sides:
-        count = lax.axis_size(axis)
-        forward = [(i, i + 1) for i in range(count - 1)]
-        backward = [(target, source) for source, target in forward]
-        low = lax.ppermute(
-            lax.slice_in_dim(block, block.shape[dim] - width, None, axis=dim), axis, forward
-        )
-        high = lax.ppermute(lax.slice_in_dim(block, 0, width, axis=dim), axis, backward)
-        block = jnp.concatenate([low, block, high], axis=dim)
-    return block
-
-
-def norm_act(field, gain, bias):
-    shape = field.shape
-    grouped = field.reshape(shape[:-3] + (shape[-3] * shape[-2], GROUPS, shape[-1] // GROUPS))
-    center = jnp.mean(grouped, axis=(-3, -1), keepdims=True)
-    spread = jnp.mean((grouped - center) ** 2, axis=(-3, -1), keepdims=True)
-    normed = ((grouped - center) * lax.rsqrt(spread + 1e-05)).reshape(shape)
-    return jax.nn.silu(normed * gain + bias)
 
 
 def adam_update(gradient, master, first, second):
@@ -77,12 +53,38 @@
     return copy
 
 
-def gather_kernel(w_ref, out_ref, ring_send, ring_recv, pair_send, pair_recv, x_send, x_recv):
+def frame_peers(t):
+    me = lax.axis_index("blk")
+    return (me, lax.rem(t + 15, 16)), (me, lax.rem(t + 1, 16))
+
+
+def send_edges(frames, edges, send_sem, recv_sem, low, high):
+    return [
+        send(frames.at[0], edges.at[1], send_sem.at[1], recv_sem.at[1], low),
+        send(frames.at[1], edges.at[0], send_sem.at[0], recv_sem.at[0], high),
+    ]
+
+
+def gather_kernel(
+    w_ref,
+    cot_ref,
+    out_ref,
+    edge_ref,
+    ring_send,
+    ring_recv,
+    pair_send,
+    pair_recv,
+    x_send,
+    x_recv,
+    edge_send,
+    edge_recv,
+):
     x, y, c, t = place()
     partner = (owner(x, y, 1 - c), t)
     across = (owner(1 - x, y, c), t)
     ring = ((owner(x, y + 1, c), t), (owner(x, y - 1, c), t))
-    greet([partner, across, ring[0], ring[1]])
+    low, high = frame_peers(t)
+    greet([partner, across, ring[0], ring[1], low, high])
     started = []
 
     def pass_on(src, k, offset):
@@ -103,6 +105,8 @@
     for d in range(2):
         copies[d, 0] = hop(w_ref, d, 0, 0)
     pass_on(w_ref, 0, 0)
+    edges = send_edges(cot_ref, edge_ref, edge_send, edge_recv, low, high)
+    started.extend(edges)
     out_ref[mine] = w_ref[...]
     x_copy.wait_recv()
     other = out_ref.at[owner(1 - x, y, c)]
@@ -134,19 +138,33 @@
             device_id=partner,
             device_id_type=MESH,
         ).wait_recv()
-
-
-def gather_weights(rows):
+    for copy in edges:
+        copy.wait_recv()
+
+
+def gather_weights(rows, cotangent):
     dma = pltpu.SemaphoreType.DMA
     return pl.pallas_call(
         gather_kernel,
-        out_shape=jax.ShapeDtypeStruct((32,) + rows.shape, rows.dtype),
-        in_specs=[VMEM],
-        out_specs=VMEM,
-        scratch_shapes=[dma((2, 4, 2)), dma((2, 4, 2)), dma((16,)), dma((16,)), dma(()), dma(())],
+        out_shape=(
+            jax.ShapeDtypeStruct((32,) + rows.shape, rows.dtype),
+            jax.ShapeDtypeStruct(cotangent.shape, cotangent.dtype),
+        ),
+        in_specs=[VMEM, VMEM],
+        out_specs=(VMEM, VMEM),
+        scratch_shapes=[
+            dma((2, 4, 2)),
+            dma((2, 4, 2)),
+            dma((16,)),
+            dma((16,)),
+            dma(()),
+            dma(()),
+            dma((2,)),
+            dma((2,)),
+        ],
         compiler_params=pltpu.CompilerParams(collective_id=0, has_side_effects=True),
         name="gather_weights",
-    )(rows)
+    )(rows, cotangent)
 
 
 PAIR_ORDER = (4, 3, -3, 2, -2, 1, -1, 0)
@@ -155,8 +173,10 @@
 def reduce_kernel(
     g_ref,
     n_ref,
+    space_ref,
     out_ref,
     norm_ref,
+    edge_ref,
     pair_buf,
     ring_src,
     ring_dst,
@@ -190,6 +210,8 @@
     ny_r,
     nz_s,
     nz_r,
+    edge_s,
+    edge_r,
 ):
     f32 = jnp.float32
     x, y, c, t = place()
@@ -201,7 +223,8 @@
     y_peers = [(owner(x, y + i, c), t) for i in range(1, 8)]
     z_peers = [(mine, lax.rem(z + i, 8) * 2 + h) for i in range(1, 8)]
     ring = (y_peers[0], y_peers[6])
-    greet([partner, across, far] + y_peers + z_peers)
+    low, high = frame_peers(t)
+    greet([partner, across, far, low, high] + y_peers + z_peers)
     started = []
 
     def go(*args):
@@ -216,6 +239,8 @@
         pair.append(
             go(g_ref.at[:, target, 1 - c], pair_buf.at[m], pair_s.at[m], pair_r.at[m], partner)
         )
+    edges = send_edges(space_ref, edge_ref, edge_s, edge_r, low, high)
+    started.extend(edges)
     arrived = {}
     waited = set()
 
@@ -314,13 +339,13 @@
     spread = [
         go(z_src, out_ref.at[z], zg_s.at[i], zg_r.at[i], peer) for i, peer in enumerate(z_peers)
     ]
-    for copy in spread:
+    for copy in spread + edges:
         copy.wait_recv()
     for copy in started:
         copy.wait_send()
 
 
-def reduce_gradient(gradient, norms):
+def reduce_gradient(gradient, norms, space):
     f32, bf16 = jnp.float32, jnp.bfloat16
     dma, vmem = pltpu.SemaphoreType.DMA, pltpu.VMEM
     small = vmem((8, 128), f32)
@@ -330,9 +355,10 @@
         out_shape=(
             jax.ShapeDtypeStruct((8, 24, 128), f32),
             jax.ShapeDtypeStruct((8, 128), f32),
+            jax.ShapeDtypeStruct(space.shape, space.dtype),
         ),
-        in_specs=[VMEM, VMEM],
-        out_specs=(VMEM, VMEM),
+        in_specs=[VMEM, VMEM, VMEM],
+        out_specs=(VMEM, VMEM, VMEM),
         scratch_shapes=[
             vmem((8, 2, 96, 256), f32),
             vmem((2, 4, 2, 96, 256), bf16),
@@ -367,93 +393,255 @@
             dma((7,)),
             dma((7,)),
             dma((7,)),
+            dma((2,)),
+            dma((2,)),
         ],
         compiler_params=pltpu.CompilerParams(
             collective_id=1, has_side_effects=True, vmem_limit_bytes=40 * 2**20
         ),
         name="reduce_gradient",
-    )(gradient.reshape(2, 8, 2, 96, 256), norms)
+    )(gradient.reshape(2, 8, 2, 96, 256), norms, space)
+
+
+PITCH = 48
+ROWS = 16 * PITCH
+TALL = ROWS + 2 * PITCH
+CHUNK = 2 * PITCH
+
+
+def group_mean(row):
+    rows = lax.broadcasted_iota(jnp.int32, (256, 256), 0) // 8
+    columns = lax.broadcasted_iota(jnp.int32, (256, 256), 1) // 8
+    same = (rows == columns).astype(jnp.float32)
+    total = jnp.dot(
+        jnp.broadcast_to(row, (8, 256)),
+        same,
+        precision=lax.Precision.HIGHEST,
+        preferred_element_type=jnp.float32,
+    )
+    return total[0:1] * (1.0 / (16 * 36 * 8))
+
+
+def block_kernel(
+    clip_ref,
+    cot_ref,
+    edge_ref,
+    w_ref,
+    gain_ref,
+    bias_ref,
+    space_ref,
+    input_ref,
+    g_ref,
+    norm_ref,
+    cot_pad,
+    wide,
+    tall,
+    hat,
+    back,
+    act,
+    grad,
+    flip,
+    space,
+):
+    f32, bf16 = jnp.float32, jnp.bfloat16
+    t = lax.axis_index("tm")
+    gain, bias = gain_ref[...], bias_ref[...]
+    inside = (lax.broadcasted_iota(jnp.int32, (2, PITCH, 256), 1) < 36).reshape(CHUNK, 256)
+
+    def dot(a, b, contract=(1, 0)):
+        dims = (((contract[0],), (contract[1],)), ((), ()))
+        return lax.dot_general(a, b, dims, preferred_element_type=f32)
+
+    def shift(target, f):
+        for j in range(3):
+            for start in range(0, TALL, CHUNK):
+                target[f, start : start + CHUNK, j * 256 : (j + 1) * 256] = tall[
+                    start + 7 + j : start + 7 + j + CHUNK
+                ].astype(bf16)
+
+    cot_pad[...] = jnp.zeros_like(cot_pad)
+    wide[...] = jnp.zeros_like(wide)
+    tall[...] = jnp.zeros_like(tall)
+    cot_pad[0, :, :36] = jnp.where(t == 0, 0.0, edge_ref[0].astype(f32)).astype(bf16)
+    cot_pad[1, :, :36] = cot_ref[0]
+    cot_pad[2, :, :36] = cot_ref[1]
+    cot_pad[3, :, :36] = jnp.where(t == 15, 0.0, edge_ref[1].astype(f32)).astype(bf16)
+    for i in range(3):
+        for j in range(3):
+            tap = 3 * i + j
+            slot = 3 * i + 2 - j
+            flip[slot * 256 : (slot + 1) * 256] = w_ref[tap * 256 : (tap + 1) * 256].T
+
+    def body(start):
+        return pl.ds(pl.multiple_of(start * CHUNK, CHUNK), CHUNK)
+
+    def above(start):
+        return pl.ds(pl.multiple_of(start * CHUNK + PITCH + 8, 8), CHUNK)
+
+    def folded(value):
+        return jnp.sum(value.reshape(CHUNK // 8, 8, 256), axis=0)
+
+    def field(i):
+        return wide[pl.ds(i * 2, 2)].reshape(CHUNK, 256)
+
+    zero = jnp.zeros((8, 256), f32)
+    inverse = []
+    for f in range(2):
+        wide[:, :36] = clip_ref[f].astype(f32)
+        total = lax.fori_loop(0, 8, lambda i, carry: carry + folded(field(i)), zero)
+        center = group_mean(jnp.sum(total, axis=0, keepdims=True))
+
+        def squares(i, carry):
+            value = jnp.where(inside, field(i) - center, 0.0)
+            return carry + folded(value * value)
+
+        total = lax.fori_loop(0, 8, squares, zero)
+        spread = group_mean(jnp.sum(total, axis=0, keepdims=True))
+        scale = lax.rsqrt(spread + 1e-05)
+        inverse.append(scale)
+
+        def activate(i, carry):
+            normed = jnp.where(inside, (field(i) - center) * scale, 0.0)
+            hat[f, body(i)] = normed
+            u = normed * gain + bias
+            value = jnp.where(inside, u / (1.0 + jnp.exp(-u)), 0.0)
+            tall[above(i)] = value
+            return carry
+
+        lax.fori_loop(0, 8, activate, 0)
+        shift(act, f)
+
+    for f in range(2):
+        total = dot(act[f, 0:ROWS], w_ref[0:768])
+        for i in range(1, 3):
+            total = total + dot(act[f, i * PITCH : i * PITCH + ROWS], w_ref[i * 768 : (i + 1) * 768])
+        rounded = total.astype(bf16)
+        space[f] = rounded
+        space_ref[f] = rounded.reshape(16, PITCH, 256)[:, :36]
+
+    for f in range(2):
+        total = None
+        for k in range(3):
+            tap = w_ref[(9 + k) * 256 : (10 + k) * 256]
+            term = dot(cot_pad[f + 2 - k].reshape(ROWS, 256), tap, (1, 1))
+            total = term if total is None else total + term
+        tall[PITCH + 8 : PITCH + 8 + ROWS] = total.astype(bf16).astype(f32)
+        shift(grad, f)
+
+    for k in range(3):
+        total = None
+        for f in range(2):
+            term = dot(space[f], cot_pad[f + 2 - k].reshape(ROWS, 256), (0, 0))
+            total = term if total is None else total + term
+        g_ref[(9 + k) * 256 : (10 + k) * 256] = total
+    for i in range(3):
+        total = None
+        for f in range(2):
+            term = dot(
+                act[f, i * PITCH : i * PITCH + ROWS],
+                grad[f, PITCH : PITCH + ROWS, 256:512],
+                (0, 0),
+            )
+            total = term if total is None else total + term
+        g_ref[i * 768 : (i + 1) * 768] = total
+
+    gain_sum, bias_sum = zero, zero
+    for f in range(2):
+        total = None
+        for i in range(3):
+            low = (2 - i) * PITCH
+            term = dot(grad[f, low : low + ROWS], flip[i * 768 : (i + 1) * 768])
+            total = term if total is None else total + term
+        back[...] = total
+
+        def pull(i, carry):
+            normed = hat[f, body(i)]
+            u = normed * gain + bias
+            gate = 1.0 / (1.0 + jnp.exp(-u))
+            down = jnp.where(inside, back[body(i)] * (gate * (1.0 + u * (1.0 - gate))), 0.0)
+            back[body(i)] = down
+            return carry[0] + folded(down), carry[1] + folded(down * normed)
+
+        plain, weighted = lax.fori_loop(0, 8, pull, (zero, zero))
+        bias_sum, gain_sum = bias_sum + plain, gain_sum + weighted
+        plain = group_mean(gain * jnp.sum(plain, axis=0, keepdims=True))
+        weighted = group_mean(gain * jnp.sum(weighted, axis=0, keepdims=True))
+        scale = inverse[f]
+
+        def finish(i, carry):
+            term = scale * (back[body(i)] * gain - plain - hat[f, body(i)] * weighted)
+            pair = cot_pad[f + 1, pl.ds(i * 2, 2)].reshape(CHUNK, 256)
+            result = (pair.astype(f32) + term).reshape(2, PITCH, 256)[:, :36]
+            input_ref[f, pl.ds(i * 2, 2)] = result.astype(bf16)
+            return carry
+
+        lax.fori_loop(0, 8, finish, 0)
+    norm_ref[0:1] = jnp.sum(gain_sum, axis=0, keepdims=True)
+    norm_ref[1:2] = jnp.sum(bias_sum, axis=0, keepdims=True)
+
+
+def block(clips, cotangent, edges, weights, gain, bias):
+    f32, bf16 = jnp.float32, jnp.bfloat16
+    vmem = pltpu.VMEM
+    return pl.pallas_call(
+        block_kernel,
+        out_shape=(
+            jax.ShapeDtypeStruct(clips.shape, bf16),
+            jax.ShapeDtypeStruct(clips.shape, bf16),
+            jax.ShapeDtypeStruct(weights.shape, f32),
+            jax.ShapeDtypeStruct((2, 256), f32),
+        ),
+        in_specs=[VMEM] * 6,
+        out_specs=(VMEM,) * 4,
+        scratch_shapes=[
+            vmem((4, 16, PITCH, 256), bf16),
+            vmem((16, PITCH, 256), f32),
+            vmem((TALL + 16, 256), f32),
+            vmem((2, ROWS, 256), f32),
+            vmem((ROWS, 256), f32),
+            vmem((2, TALL, 768), bf16),
+            vmem((2, TALL, 768), bf16),
+            vmem((2304, 256), bf16),
+            vmem((2, ROWS, 256), bf16),
+        ],
+        compiler_params=pltpu.CompilerParams(vmem_limit_bytes=56 * 2**20),
+        name="block",
+    )(clips, cotangent, edges, weights, gain.reshape(1, 256), bias.reshape(1, 256))
 
 
 def shards(clips, cotangent, conv_master, first_moment, second_moment, norm_gain, norm_bias):
     f32 = jnp.float32
-    frames, height, width, channels = (
-        clips.shape[1],
-        clips.shape[2],
-        clips.shape[3],
-        clips.shape[4],
+    channels = clips.shape[-1]
+    clip, cot = clips[0], cotangent[0]
+    rows, edges = gather_weights(conv_master.astype(jnp.bfloat16), cot)
+    weights = rows.reshape(12 * channels, channels)
+    space, input_grad, local_gradient, norms = block(
+        clip, cot, edges, weights, norm_gain, norm_bias
     )
-    weights = gather_weights(conv_master.astype(jnp.bfloat16)).reshape(12 * channels, channels)
-    inputs32 = clips.astype(f32)
-    act32, pullback = jax.vjp(norm_act, inputs32, norm_gain, norm_bias)
-    act = act32.astype(jnp.bfloat16)
-    act_padded = jnp.pad(act, ((0, 0), (0, 0), (1, 1), (1, 1), (0, 0)))
-    space32 = jnp.zeros(clips.shape, f32)
-    for row_tap in range(3):
-        for col_tap in range(3):
-            tap_index = 3 * row_tap + col_tap
-            window = act_padded[:, :, row_tap : row_tap + height, col_tap : col_tap + width, :]
-            tap = weights[tap_index * channels : (tap_index + 1) * channels]
-            space32 = space32 + jnp.einsum(
-                "bfhwc,cd->bfhwd", window, tap, preferred_element_type=f32
-            )
-    space = space32.astype(jnp.bfloat16)
-    space_padded = extended(space, (("tm", 1),), 1)
-    temporal = jnp.zeros(clips.shape, f32)
+    norms = jnp.pad(norms.reshape(4, 128), ((0, 4), (0, 0)))
+    pieces, norm_sums, around = reduce_gradient(local_gradient, norms, space)
+    norm_grads = norm_sums[:4].reshape(2, channels)
+    gradient = pieces.reshape(4, 2, 24, 128).transpose(0, 2, 1, 3).reshape(96, channels)
+    t = lax.axis_index("tm")
+    zero = jnp.zeros_like(around[:1])
+    padded = jnp.concatenate(
+        [
+            jnp.where(t == 0, zero, around[:1]),
+            space,
+            jnp.where(t == lax.axis_size("tm") - 1, zero, around[1:]),
+        ]
+    )
+    temporal = clip.astype(f32)
     for frame_tap in range(3):
         tap = weights[(9 + frame_tap) * channels : (10 + frame_tap) * channels]
         temporal = temporal + jnp.einsum(
-            "bfhwc,cd->bfhwd",
-            space_padded[:, frame_tap : frame_tap + frames],
+            "fhwc,cd->fhwd",
+            padded[frame_tap : frame_tap + 2],
             tap,
             preferred_element_type=f32,
         )
-    block_out = (inputs32 + temporal).astype(jnp.bfloat16)
-    back_weights = weights
-    grad_padded = extended(cotangent, (("tm", 1),), 1)
-    space_grad32 = jnp.zeros(clips.shape, f32)
-    temporal_grads = []
-    for frame_tap in range(3):
-        tap = back_weights[(9 + frame_tap) * channels : (10 + frame_tap) * channels]
-        space_grad32 = space_grad32 + jnp.einsum(
-            "bfhwd,cd->bfhwc",
-            grad_padded[:, 2 - frame_tap : 2 - frame_tap + frames],
-            tap,
-            preferred_element_type=f32,
-        )
-        temporal_grads.append(
-            jnp.einsum(
-                "bfhwc,bfhwd->cd",
-                space,
-                grad_padded[:, 2 - frame_tap : 2 - frame_tap + frames],
-                preferred_element_type=f32,
-            )
-        )
-    space_grad = space_grad32.astype(jnp.bfloat16)
-    sgrad_padded = jnp.pad(space_grad, ((0, 0), (0, 0), (1, 1), (1, 1), (0, 0)))
-    act_grad = jnp.zeros(clips.shape, f32)
-    spatial_grads = []
-    for row_tap in range(3):
-        for col_tap in range(3):
-            tap_index = 3 * row_tap + col_tap
-            tap = back_weights[tap_index * channels : (tap_index + 1) * channels]
-            window = act_padded[:, :, row_tap : row_tap + height, col_tap : col_tap + width, :]
-            spatial_grads.append(
-                jnp.einsum("bfhwc,bfhwd->cd", window, space_grad, preferred_element_type=f32)
-            )
-            back_window = sgrad_padded[
-                :, :, 2 - row_tap : 2 - row_tap + height, 2 - col_tap : 2 - col_tap + width, :
-            ]
-            act_grad = act_grad + jnp.einsum(
-                "bfhwd,cd->bfhwc", back_window, tap, preferred_element_type=f32
-            )
-    input_term, gain_grad, bias_grad = pullback(act_grad)
-    input_grad = (cotangent.astype(f32) + input_term).astype(jnp.bfloat16)
-    local_gradient = jnp.concatenate(spatial_grads + temporal_grads, axis=0)
-    norms = jnp.pad(jnp.concatenate([gain_grad, bias_grad]).reshape(4, 128), ((0, 4), (0, 0)))
-    pieces, norm_sums = reduce_gradient(local_gradient, norms)
-    norm_grads = norm_sums[:4].reshape(2, channels)
-    gradient = pieces.reshape(4, 2, 24, 128).transpose(0, 2, 1, 3).reshape(96, channels)
+    block_out = temporal.astype(jnp.bfloat16)[None]
+    input_grad = input_grad[None]
     new_master, new_first, new_second = adam_update(
         gradient, conv_master, first_moment, second_moment
     )

time: 135 us -> 118 us (0.87)
  the two profiles are of different devices: /device:TPU:18 before, /device:TPU:8 now
where the time goes in v2:
time: 118 us
  Pallas kernels  103 us (87%)
  local copies, waits for them, and re-layouts  9 us (8%)
  matrix products  3.82 us (3%)
  other arithmetic  1.42 us (1%)
    pallas_call x1, Pallas kernels, reduce_gradient(): pl.pallas_call(reduce_kernel, out_shape=(jax.ShapeDtypeStruct((8, 24, 128...  48.4 us
    pallas_call x1, Pallas kernels, gather_weights(): pl.pallas_call(gather_kernel, out_shape=(jax.ShapeDtypeStruct((32,) + row...  35.2 us
    pallas_call x1, Pallas kernels, block(): pl.pallas_call(block_kernel, out_shape=(jax.ShapeDtypeStruct(clips.shape,...  18.9 us
    unnamed x18, local copies, waits for them, and re-layouts  4.86 us
    dot_general x3, matrix products, shards(): jnp.einsum('fhwc,cd->fhwd', padded[frame_tap:frame_tap + 2], tap, preferr...  3.82 us
    squeeze x1, local copies, waits for them, and re-layouts, shards(): clip, cot = (clips[0], cotangent[0])  2.8 us

profile of v2, /device:TPU:8, one launch (start us, length us, event | category | flops | bytes accessed | tf_op | source)
XLA Modules:
  0.0 117.5 jit_solution(1582683102409989258)
XLA Ops:
  0.6 0.0 copy-start.5
  0.6 2.8 %copy_bitcast_fusion = (bf16[2,16,36,256]{3,2,1,0:T(8,128)(2,1)}, bf16[2,16,36,256]{3,2,1,0:T(8,128)(2,1)}) fusion(bf16[1,2,16,36,256]{4,2,3,1,0:T(8,128)(2,1)} %param.8, bf16[1,2,16,36,256]{4,2,3,1,0:T(8,128)(2,1)} %param.7), kind=kLoop, calls=%fused_computation.12 | loop fusion | bytes 2359296 | tf_op jit(solution)/shard_map/squeeze | solution.py:615
  3.4 0.0 copy-done.5
  3.4 0.6 convert_element_type.12.w_ref
  4.1 35.2 %gather_weights.1 = (bf16[32,96,256]{2,1,0:T(8,128)(2,1)}, bf16[2,16,36,256]{3,2,1,0:T(8,128)(2,1)}) custom-call(bf16[96,256]{1,0:T(8,128)(2,1)} %convert_element_type.12.w_ref, bf16[2,16,36,256]{3,2,1,0:T(8,128)(2,1)} %get-tuple-element.35.cot_ref), custom_call_target="tpu_custom_call" | custom-call | tf_op jit(solution)/shard_map/gather_weights/pallas_call | solution.py:147
  39.3 18.9 %block.1 = (bf16[2,16,36,256]{3,2,1,0:T(8,128)(2,1)}, bf16[2,16,36,256]{3,2,1,0:T(8,128)(2,1)}, f32[3072,256]{1,0:T(8,128)}, f32[2,256]{1,0:T(2,128)}) custom-call(bf16[2,16,36,256]{3,2,1,0:T(8,128)(2,1)} %get-tuple-element.36.clip_ref, bf16[2,16,36,256]{3,2,1,0:T(8,128)(2,1)} %get-tuple-element.35.cot_ref, ...), custom_call_target="tpu_custom_call" | custom-call | tf_op jit(solution)/shard_map/block/pallas_call | solution.py:586
  58.2 0.7 reshape.40
  58.9 0.0 copy-start
  58.9 1.1 copy-done
  60.0 0.0 copy-start.2
  60.0 1.9 %copy-done.2 = f32[3072,256]{1,0:T(8,128)S(1)} copy-done((f32[3072,256]{1,0:T(8,128)S(1)}, f32[3072,256]{1,0:T(8,128)}, u32[]{:S(2)}) %copy-start.2) | copy-done | bytes 3145752
  61.8 0.0 copy-start.1
  61.9 0.0 copy-start.3
  61.9 48.4 %reduce_gradient.1 = (f32[8,24,128]{2,1,0:T(8,128)S(1)}, f32[8,128]{1,0:T(8,128)S(1)}, bf16[2,16,36,256]{3,2,1,0:T(8,128)(2,1)S(1)}) custom-call(f32[2,8,2,96,256]{4,3,2,1,0:T(8,128)S(1)} %bitcast.41, f32[8,128]{1,0:T(8,128)S(1)} %pad.4.n_ref, bf16[2,16,36,256]{3,2,1,0:T(8,128)(2,1)S(1)} %copy-done), custom_call_target="tpu_custom_call" | custom-call | tf_op jit(solution)/shard_map/reduce_gradient/pallas_call | solution.py:353
  110.4 0.0 copy-done.1
  110.4 0.0 copy-done.3
  110.4 1.3 %convolution_add_fusion.1 = f32[2,16,36,256]{3,2,1,0:T(8,128)S(1)} fusion(bf16[2,16,36,256]{3,2,1,0:T(8,128)(2,1)S(1)} %copy-done.1, bf16[1,16,36,256]{3,2,1,0:T(8,128)(2,1)S(1)} %get-tuple-element.33, bf16[3072,256]{1,0:T(8,128)(2,1)} %bitcast.44, bf16[1,2,16,36,256]{4,2,3,1,0:T(8,128)(2,1)S(1)} %copy-done.3), kind=kOutput, calls=%fused_computation.2 | convolution fusion | flops 153354240 | bytes 2785280 | tf_op jit(solution)/shard_map/fhwc,cd->fhwd/dot_general | solution.py:637
  111.7 1.3 %fusion.6 = f32[2,16,36,256]{3,2,1,0:T(8,128)S(1)} fusion(bf16[1,16,36,256]{3,2,1,0:T(8,128)(2,1)S(1)} %get-tuple-element.34, bf16[2,16,36,256]{3,2,1,0:T(8,128)(2,1)S(1)} %copy-done.1, bf16[3072,256]{1,0:T(8,128)(2,1)} %bitcast.45), kind=kOutput, calls=%fused_computation.8 | convolution fusion | flops 152764416 | bytes 2195456 | tf_op jit(solution)/shard_map/fhwc,cd->fhwd/dot_general | solution.py:637
  112.9 0.0 copy-start.6
  112.9 0.0 copy-start.7
  113.0 1.3 %fusion.2 = bf16[1,2,16,36,256]{4,3,2,1,0:T(8,128)(2,1)S(1)} fusion(f32[2,16,36,256]{3,2,1,0:T(8,128)S(1)} %fusion.6, f32[2,16,36,256]{3,2,1,0:T(8,128)S(1)} %convolution_add_fusion.1, bf16[2,16,36,256]{3,2,1,0:T(8,128)(2,1)S(1)} %copy-done.1, bf16[3072,256]{1,0:T(8,128)(2,1)} %bitcast.46), kind=kOutput, calls=%fused_computation.4 | convolution fusion | flops 151879680 | bytes 3670016 | tf_op jit(solution)/shard_map/fhwc,cd->fhwd/dot_general | solution.py:637
  114.2 0.0 copy-start.4
  114.3 0.9 copy.16
  115.2 0.1 copy.15
  115.2 0.0 copy-done.6
  115.2 0.0 copy-done.7
  115.3 0.7 multiply_subtract_fusion
  116.0 0.6 reshape.43
  116.6 0.0 copy-done.4
  116.6 0.9 copy.17
  (3 shorter events, 0.1 us)
Async XLA Ops:
  0.6 2.8 %copy-start.5 = (f32[96,256]{1,0:T(8,128)S(1)}, f32[96,256]{1,0:T(8,128)}, u32[]{:S(2)}) copy-start(f32[96,256]{1,0:T(8,128)} %param.9) | copy-start | bytes 294916
  58.9 1.1 copy-start
  60.0 1.9 %copy-start.2 = (f32[3072,256]{1,0:T(8,128)S(1)}, f32[3072,256]{1,0:T(8,128)}, u32[]{:S(2)}) copy-start(f32[3072,256]{1,0:T(8,128)} %get-tuple-element.17) | copy-start | bytes 9437188
  61.8 48.5 %copy-start.1 = (bf16[2,16,36,256]{3,2,1,0:T(8,128)(2,1)S(1)}, bf16[2,16,36,256]{3,2,1,0:T(8,128)(2,1)}, u32[]{:S(2)}) copy-start(bf16[2,16,36,256]{3,2,1,0:T(8,128)(2,1)} %get-tuple-element.19.space_ref) | copy-start | bytes 1769476
  61.9 48.5 %copy-start.3 = (bf16[1,2,16,36,256]{4,2,3,1,0:T(8,128)(2,1)S(1)}, bf16[1,2,16,36,256]{4,2,3,1,0:T(8,128)(2,1)}, u32[]{:S(2)}) copy-start(bf16[1,2,16,36,256]{4,2,3,1,0:T(8,128)(2,1)} %param.7) | copy-start | bytes 1769476
  112.9 2.3 %copy-start.6 = (f32[96,256]{1,0:T(8,128)S(1)}, f32[96,256]{1,0:T(8,128)}, u32[]{:S(2)}) copy-start(f32[96,256]{1,0:T(8,128)} %param.10) | copy-start | bytes 294916
  112.9 2.3 %copy-start.7 = (f32[96,256]{1,0:T(8,128)S(1)}, f32[96,256]{1,0:T(8,128)}, u32[]{:S(2)}) copy-start(f32[96,256]{1,0:T(8,128)} %param.11) | copy-start | bytes 294916
  114.2 2.4 %copy-start.4 = (bf16[2,16,36,256]{3,2,1,0:T(8,128)(2,1)S(1)}, bf16[2,16,36,256]{3,2,1,0:T(8,128)(2,1)}, u32[]{:S(2)}) copy-start(bf16[2,16,36,256]{3,2,1,0:T(8,128)(2,1)} %get-tuple-element.21) | copy-start | bytes 1769476

commit v3 on v2

--- a/solution.py
+++ b/solution.py
@@ -53,16 +53,69 @@
     return copy
 
 
-def frame_peers(t):
-    me = lax.axis_index("blk")
-    return (me, lax.rem(t + 15, 16)), (me, lax.rem(t + 1, 16))
-
-
-def send_edges(frames, edges, send_sem, recv_sem, low, high):
-    return [
-        send(frames.at[0], edges.at[1], send_sem.at[1], recv_sem.at[1], low),
-        send(frames.at[1], edges.at[0], send_sem.at[0], recv_sem.at[0], high),
-    ]
+def at_chip(position, y, c, t):
+    position = lax.rem(position + 4, 4)
+    t = lax.rem(t + 16, 16)
+    return owner(lax.rem(position, 2), y, c), (t // 2) * 2 + position // 2
+
+
+class Edges:
+    def __init__(self, frames, edges, relay, sems):
+        self.frames, self.edges, self.relay, self.sems = frames, edges, relay, sems
+        x, y, c, t = place()
+        here = lax.rem(t, 2) * 2 + x
+        self.near, self.last, self.source = [], [], []
+        for step in (1, -1):
+            z = t // 2
+            origin = lax.rem(here - step + 4, 4)
+            t_origin = z * 2 + origin // 2
+            t_last = lax.rem(t_origin + step + 16, 16)
+            self.near.append(at_chip(here + step, y, c, t))
+            self.last.append((owner(lax.rem(origin, 2), y, c), t_last))
+            self.source.append(at_chip(here - step, y, c, t - step))
+
+    def signalled(self):
+        return self.near + self.source
+
+    def start(self):
+        first_s, first_r, _, _ = self.sems
+        self.first, self.second = {}, []
+        for q in range(4):
+            for d in range(2):
+                rows = pl.ds(q * 4, 4)
+                self.first[d, q] = send(
+                    self.frames.at[1 - d, rows],
+                    self.relay.at[d, rows],
+                    first_s.at[d, q],
+                    first_r.at[d, q],
+                    self.near[d],
+                )
+
+    def forward(self, q):
+        _, _, second_s, second_r = self.sems
+        for d in range(2):
+            rows = pl.ds(q * 4, 4)
+            self.first[d, q].wait_recv()
+            self.second.append(
+                send(
+                    self.relay.at[d, rows],
+                    self.edges.at[d, rows],
+                    second_s.at[d, q],
+                    second_r.at[d, q],
+                    self.last[d],
+                )
+            )
+
+    def finish(self):
+        for copy in self.second:
+            copy.wait()
+        for copy in self.first.values():
+            copy.wait_send()
+
+
+def edge_scratch(frames):
+    dma = pltpu.SemaphoreType.DMA
+    return [pltpu.VMEM(frames.shape, frames.dtype)] + [dma((2, 4))] * 4
 
 
 def gather_kernel(
@@ -76,15 +129,15 @@
     pair_recv,
     x_send,
     x_recv,
-    edge_send,
-    edge_recv,
+    relay,
+    *edge_sems,
 ):
     x, y, c, t = place()
     partner = (owner(x, y, 1 - c), t)
     across = (owner(1 - x, y, c), t)
     ring = ((owner(x, y + 1, c), t), (owner(x, y - 1, c), t))
-    low, high = frame_peers(t)
-    greet([partner, across, ring[0], ring[1], low, high])
+    edges = Edges(cot_ref, edge_ref, relay, edge_sems)
+    greet([partner, across, ring[0], ring[1]] + edges.signalled())
     started = []
 
     def pass_on(src, k, offset):
@@ -105,8 +158,7 @@
     for d in range(2):
         copies[d, 0] = hop(w_ref, d, 0, 0)
     pass_on(w_ref, 0, 0)
-    edges = send_edges(cot_ref, edge_ref, edge_send, edge_recv, low, high)
-    started.extend(edges)
+    edges.start()
     out_ref[mine] = w_ref[...]
     x_copy.wait_recv()
     other = out_ref.at[owner(1 - x, y, c)]
@@ -124,6 +176,7 @@
                 if s < 3 or (s == 3 and k == d):
                     copies[d, k] = hop(block, d, s, k)
                 pass_on(block, k, offset)
+        edges.forward(s - 1)
     x_copy.wait_send()
     for copy in started:
         copy.wait_send()
@@ -138,8 +191,7 @@
             device_id=partner,
             device_id_type=MESH,
         ).wait_recv()
-    for copy in edges:
-        copy.wait_recv()
+    edges.finish()
 
 
 def gather_weights(rows, cotangent):
@@ -159,10 +211,11 @@
             dma((16,)),
             dma(()),
             dma(()),
-            dma((2,)),
-            dma((2,)),
-        ],
-        compiler_params=pltpu.CompilerParams(collective_id=0, has_side_effects=True),
+        ]
+        + edge_scratch(cotangent),
+        compiler_params=pltpu.CompilerParams(
+            collective_id=0, has_side_effects=True, vmem_limit_bytes=10 * 2**20
+        ),
         name="gather_weights",
     )(rows, cotangent)
 
@@ -210,8 +263,8 @@
     ny_r,
     nz_s,
     nz_r,
-    edge_s,
-    edge_r,
+    relay,
+    *edge_sems,
 ):
     f32 = jnp.float32
     x, y, c, t = place()
@@ -223,8 +276,8 @@
     y_peers = [(owner(x, y + i, c), t) for i in range(1, 8)]
     z_peers = [(mine, lax.rem(z + i, 8) * 2 + h) for i in range(1, 8)]
     ring = (y_peers[0], y_peers[6])
-    low, high = frame_peers(t)
-    greet([partner, across, far, low, high] + y_peers + z_peers)
+    edges = Edges(space_ref, edge_ref, relay, edge_sems)
+    greet([partner, across, far] + y_peers + z_peers + edges.signalled())
     started = []
 
     def go(*args):
@@ -239,8 +292,7 @@
         pair.append(
             go(g_ref.at[:, target, 1 - c], pair_buf.at[m], pair_s.at[m], pair_r.at[m], partner)
         )
-    edges = send_edges(space_ref, edge_ref, edge_s, edge_r, low, high)
-    started.extend(edges)
+    edges.start()
     arrived = {}
     waited = set()
 
@@ -303,6 +355,7 @@
                 part = part + n_z[i]
             n_h_src[...] = part
             norm_h = go(n_h_src, n_h, one_s.at[2], one_r.at[2], far)
+        edges.forward(s)
 
     totals = []
     for k in range(2):
@@ -339,8 +392,9 @@
     spread = [
         go(z_src, out_ref.at[z], zg_s.at[i], zg_r.at[i], peer) for i, peer in enumerate(z_peers)
     ]
-    for copy in spread + edges:
+    for copy in spread:
         copy.wait_recv()
+    edges.finish()
     for copy in started:
         copy.wait_send()
 
@@ -393,11 +447,10 @@
             dma((7,)),
             dma((7,)),
             dma((7,)),
-            dma((2,)),
-            dma((2,)),
-        ],
+        ]
+        + edge_scratch(space),
         compiler_params=pltpu.CompilerParams(
-            collective_id=1, has_side_effects=True, vmem_limit_bytes=40 * 2**20
+            collective_id=1, has_side_effects=True, vmem_limit_bytes=18 * 2**20
         ),
         name="reduce_gradient",
     )(gradient.reshape(2, 8, 2, 96, 256), norms, space)
@@ -604,7 +657,7 @@
             vmem((2304, 256), bf16),
             vmem((2, ROWS, 256), bf16),
         ],
-        compiler_params=pltpu.CompilerParams(vmem_limit_bytes=56 * 2**20),
+        compiler_params=pltpu.CompilerParams(vmem_limit_bytes=36 * 2**20),
         name="block",
     )(clips, cotangent, edges, weights, gain.reshape(1, 256), bias.reshape(1, 256))
 

time: 118 us -> 103 us (0.87)
  Pallas kernels: 103 us -> 91 us
  matrix products: 3.82 us -> 2.13 us
    pallas_call x1, Pallas kernels: 48.4 us -> 39.6 us  [reduce_gradient(): pl.pallas_call(reduce_kernel, out_shape=(jax.ShapeDtypeStruct((8, 24, 128...]
    pallas_call x1, Pallas kernels: 18.9 us -> 14.9 us  [block(): pl.pallas_call(block_kernel, out_shape=(jax.ShapeDtypeStruct(clips.shape,...]
    dot_general x3, matrix products: 3.82 us -> 2.13 us  [shards(): jnp.einsum('fhwc,cd->fhwd', padded[frame_tap:frame_tap + 2], tap, preferr...]
    pallas_call x1, Pallas kernels: 35.2 us -> 36.5 us  [gather_weights(): pl.pallas_call(gather_kernel, out_shape=(jax.ShapeDtypeStruct((32,) + row...]
    unnamed x18 -> x22, local copies, waits for them, and re-layouts: 4.86 us -> 6.05 us
where the time goes in v3:
time: 103 us
  Pallas kernels  91 us (88%)
  local copies, waits for them, and re-layouts  8.44 us (8%)
  matrix products  2.13 us (2%)
    pallas_call x1, Pallas kernels, reduce_gradient(): pl.pallas_call(reduce_kernel, out_shape=(jax.ShapeDtypeStruct((8, 24, 128...  39.6 us
    pallas_call x1, Pallas kernels, gather_weights(): pl.pallas_call(gather_kernel, out_shape=(jax.ShapeDtypeStruct((32,) + row...  36.5 us
    pallas_call x1, Pallas kernels, block(): pl.pallas_call(block_kernel, out_shape=(jax.ShapeDtypeStruct(clips.shape,...  14.9 us
    unnamed x22, local copies, waits for them, and re-layouts  6.05 us
    dot_general x3, matrix products, shards(): jnp.einsum('fhwc,cd->fhwd', padded[frame_tap:frame_tap + 2], tap, preferr...  2.13 us

profile of v3, /device:TPU:8, one launch (start us, length us, event | category | flops | bytes accessed | tf_op | source)
XLA Modules:
  0.0 103.2 jit_solution(5864852544353110436)
XLA Ops:
  0.6 0.0 copy-start.6
  0.6 0.0 copy-start.4
  0.7 0.0 copy-start.5
  0.7 1.7 %copy_bitcast_fusion = (bf16[2,16,36,256]{3,2,1,0:T(8,128)(2,1)S(1)}, bf16[2,16,36,256]{3,2,1,0:T(8,128)(2,1)S(1)}) fusion(bf16[1,2,16,36,256]{4,2,3,1,0:T(8,128)(2,1)} %param.8, bf16[1,2,16,36,256]{4,2,3,1,0:T(8,128)(2,1)} %param.7), kind=kLoop, calls=%fused_computation.12 | loop fusion | bytes 2359296 | tf_op jit(solution)/shard_map/squeeze | solution.py:668
  2.4 0.0 copy-done.6
  2.4 36.5 %gather_weights.1 = (bf16[32,96,256]{2,1,0:T(8,128)(2,1)S(1)}, bf16[2,16,36,256]{3,2,1,0:T(8,128)(2,1)S(1)}) custom-call(bf16[96,256]{1,0:T(8,128)(2,1)S(1)} %convert_element_type.12.w_ref, bf16[2,16,36,256]{3,2,1,0:T(8,128)(2,1)S(1)} %get-tuple-element.35.cot_ref), custom_call_target="tpu_custom_call" | custom-call | tf_op jit(solution)/shard_map/gather_weights/pallas_call | solution.py:199
  38.9 0.0 copy-done.4
  38.9 0.0 copy-done.5
  38.9 14.9 %block.1 = (bf16[2,16,36,256]{3,2,1,0:T(8,128)(2,1)S(1)}, bf16[2,16,36,256]{3,2,1,0:T(8,128)(2,1)S(1)}, f32[3072,256]{1,0:T(8,128)S(1)}, f32[2,256]{1,0:T(2,128)S(1)}) custom-call(bf16[2,16,36,256]{3,2,1,0:T(8,128)(2,1)S(1)} %get-tuple-element.36.clip_ref, bf16[2,16,36,256]{3,2,1,0:T(8,128)(2,1)S(1)} %get-tuple-element.35.cot_ref, ...), custom_call_target="tpu_custom_call" | custom-call | tf_op jit(solution)/shard_map/block/pallas_call | solution.py:639
  53.9 0.0 copy-start
  53.9 1.6 %copy-done = f32[3072,256]{1,0:T(8,128)} copy-done((f32[3072,256]{1,0:T(8,128)}, f32[3072,256]{1,0:T(8,128)S(1)}, u32[]{:S(2)}) %copy-start) | copy-done | bytes 3145752
  55.5 0.0 copy-start.1
  55.5 1.9 %copy-done.1 = f32[3072,256]{1,0:T(8,128)S(1)} copy-done((f32[3072,256]{1,0:T(8,128)S(1)}, f32[3072,256]{1,0:T(8,128)}, u32[]{:S(2)}) %copy-start.1) | copy-done | bytes 3145752
  57.4 39.6 %reduce_gradient.1 = (f32[8,24,128]{2,1,0:T(8,128)S(1)}, f32[8,128]{1,0:T(8,128)S(1)}, bf16[2,16,36,256]{3,2,1,0:T(8,128)(2,1)S(1)}) custom-call(f32[2,8,2,96,256]{4,3,2,1,0:T(8,128)S(1)} %bitcast.41, f32[8,128]{1,0:T(8,128)S(1)} %pad.4.n_ref, bf16[2,16,36,256]{3,2,1,0:T(8,128)(2,1)S(1)} %get-tuple-element.19.space_ref), custom_call_target="tpu_custom_call" | custom-call | tf_op jit(solution)/shard_map/reduce_gradient/pallas_call | solution.py:407
  97.0 0.0 copy-start.2
  97.1 0.6 copy-done.2
  97.7 1.4 %convolution_add_fusion.1 = f32[2,16,36,256]{3,2,1,0:T(8,128)S(1)} fusion(bf16[2,16,36,256]{3,2,1,0:T(8,128)(2,1)S(1)} %get-tuple-element.19.space_ref, bf16[1,16,36,256]{3,2,1,0:T(8,128)(2,1)S(1)} %get-tuple-element.33, bf16[3072,256]{1,0:T(8,128)(2,1)S(1)} %bitcast.43, bf16[1,2,16,36,256]{4,2,3,1,0:T(8,128)(2,1)} %param.7), kind=kOutput, calls=%fused_computation.2 | convolution fusion | flops 153354240 | bytes 2883584 | tf_op jit(solution)/shard_map/fhwc,cd->fhwd/dot_general | solution.py:690
  99.2 0.3 fusion.6
  99.5 0.0 copy-start.3
  99.5 0.0 copy-start.7
  99.6 0.0 copy-start.8
  99.6 0.0 copy-start.9
  99.6 0.3 fusion.2
  99.9 0.9 copy.16
  100.9 0.0 copy-done.3
  100.9 0.1 copy.15
  100.9 0.0 copy-done.7
  100.9 0.0 copy-done.8
  100.9 0.0 copy-done.9
  100.9 0.7 multiply_subtract_fusion
  101.7 0.6 reshape.43
  102.3 0.9 copy.17
  (5 shorter events, 0.1 us)
Async XLA Ops:
  0.6 1.8 %copy-start.6 = (f32[96,256]{1,0:T(8,128)S(1)}, f32[96,256]{1,0:T(8,128)}, u32[]{:S(2)}) copy-start(f32[96,256]{1,0:T(8,128)} %param.9) | copy-start | bytes 294916
  0.6 38.3 %copy-start.4 = (f32[256]{0:T(256)S(1)}, f32[256]{0:T(256)}, u32[]{:S(2)}) copy-start(f32[256]{0:T(256)} %param.12) | copy-start | bytes 3076
  0.7 38.3 %copy-start.5 = (f32[256]{0:T(256)S(1)}, f32[256]{0:T(256)}, u32[]{:S(2)}) copy-start(f32[256]{0:T(256)} %param.13) | copy-start | bytes 3076
  53.9 1.6 %copy-start = (f32[3072,256]{1,0:T(8,128)}, f32[3072,256]{1,0:T(8,128)S(1)}, u32[]{:S(2)}) copy-start(f32[3072,256]{1,0:T(8,128)S(1)} %get-tuple-element.17) | copy-start | bytes 9437188
  55.5 1.9 %copy-start.1 = (f32[3072,256]{1,0:T(8,128)S(1)}, f32[3072,256]{1,0:T(8,128)}, u32[]{:S(2)}) copy-start(f32[3072,256]{1,0:T(8,128)} %copy-done) | copy-start | bytes 9437188
  97.0 0.6 copy-start.2
  99.5 1.3 %copy-start.3 = (f32[8,24,128]{2,1,0:T(8,128)S(1)}, f32[8,24,128]{2,1,0:T(8,128)}, u32[]{:S(2)}) copy-start(f32[8,24,128]{2,1,0:T(8,128)} %copy-done.2) | copy-start | bytes 294916
  99.5 1.4 %copy-start.7 = (f32[96,256]{1,0:T(8,128)S(1)}, f32[96,256]{1,0:T(8,128)}, u32[]{:S(2)}) copy-start(f32[96,256]{1,0:T(8,128)} %param.9) | copy-start | bytes 294916
  99.6 1.4 %copy-start.8 = (f32[96,256]{1,0:T(8,128)S(1)}, f32[96,256]{1,0:T(8,128)}, u32[]{:S(2)}) copy-start(f32[96,256]{1,0:T(8,128)} %param.10) | copy-start | bytes 294916
  99.6 1.4 %copy-start.9 = (f32[96,256]{1,0:T(8,128)S(1)}, f32[96,256]{1,0:T(8,128)}, u32[]{:S(2)}) copy-start(f32[96,256]{1,0:T(8,128)} %param.11) | copy-start | bytes 294916

commit v4 on v3

--- a/solution.py
+++ b/solution.py
@@ -220,16 +220,96 @@
     )(rows, cotangent)
 
 
+PITCH = 48
+ROWS = 16 * PITCH
+TALL = ROWS + 2 * PITCH
+CHUNK = 2 * PITCH
+
+
+def group_mean(row):
+    rows = lax.broadcasted_iota(jnp.int32, (256, 256), 0) // 8
+    columns = lax.broadcasted_iota(jnp.int32, (256, 256), 1) // 8
+    same = (rows == columns).astype(jnp.float32)
+    total = jnp.dot(
+        jnp.broadcast_to(row, (8, 256)),
+        same,
+        precision=lax.Precision.HIGHEST,
+        preferred_element_type=jnp.float32,
+    )
+    return total[0:1] * (1.0 / (16 * 36 * 8))
+
+
+def pull_back(
+    f, cot_ref, grad_ref, flip_ref, hat_ref, scale_ref, gain_ref, bias_ref, input_ref, back, wide
+):
+    f32, bf16 = jnp.float32, jnp.bfloat16
+    gain, bias = gain_ref[...], bias_ref[...]
+    inside = (lax.broadcasted_iota(jnp.int32, (2, PITCH, 256), 1) < 36).reshape(CHUNK, 256)
+    zero = jnp.zeros((8, 256), f32)
+    total = None
+    for i in range(3):
+        low = (2 - i) * PITCH
+        term = jnp.dot(
+            grad_ref[f, low : low + ROWS],
+            flip_ref[i * 768 : (i + 1) * 768],
+            preferred_element_type=f32,
+        )
+        total = term if total is None else total + term
+    back[...] = total
+    wide[...] = jnp.zeros_like(wide)
+    wide[:, :36] = cot_ref[f]
+
+    def body(start):
+        return pl.ds(pl.multiple_of(start * CHUNK, CHUNK), CHUNK)
+
+    def folded(value):
+        return jnp.sum(value.reshape(CHUNK // 8, 8, 256), axis=0)
+
+    def pull(i, carry):
+        normed = hat_ref[f, body(i)]
+        u = normed * gain + bias
+        gate = 1.0 / (1.0 + jnp.exp(-u))
+        down = jnp.where(inside, back[body(i)] * (gate * (1.0 + u * (1.0 - gate))), 0.0)
+        back[body(i)] = down
+        return carry[0] + folded(down), carry[1] + folded(down * normed)
+
+    plain, weighted = lax.fori_loop(0, 8, pull, (zero, zero))
+    plain = jnp.sum(plain, axis=0, keepdims=True)
+    weighted = jnp.sum(weighted, axis=0, keepdims=True)
+    plain_mean, weighted_mean = group_mean(gain * plain), group_mean(gain * weighted)
+    scale = scale_ref[f : f + 1]
+
+    def finish(i, carry):
+        term = scale * (back[body(i)] * gain - plain_mean - hat_ref[f, body(i)] * weighted_mean)
+        pair = wide[pl.ds(i * 2, 2)].reshape(CHUNK, 256)
+        result = (pair.astype(f32) + term).reshape(2, PITCH, 256)[:, :36]
+        input_ref[f, pl.ds(i * 2, 2)] = result.astype(bf16)
+        return carry
+
+    lax.fori_loop(0, 8, finish, 0)
+    return plain, weighted
+
+
 PAIR_ORDER = (4, 3, -3, 2, -2, 1, -1, 0)
 
 
 def reduce_kernel(
     g_ref,
-    n_ref,
     space_ref,
+    cot_ref,
+    grad_ref,
+    flip_ref,
+    hat_ref,
+    scale_ref,
+    gain_ref,
+    bias_ref,
     out_ref,
     norm_ref,
     edge_ref,
+    input_ref,
+    back,
+    wide,
+    n_ref,
     pair_buf,
     ring_src,
     ring_dst,
@@ -285,7 +365,6 @@
         started.append(copy)
         return copy
 
-    norm_pair = go(n_ref, n_pair, one_s.at[0], one_r.at[0], partner)
     pair = []
     for m, offset in enumerate(PAIR_ORDER):
         target = lax.rem(y + offset + 8, 8)
@@ -321,7 +400,19 @@
                     ring_r.at[d, s, k],
                     ring[d],
                 )
-        if s == 0:
+        edges.forward(s)
+        if s < 2:
+            plain, weighted = pull_back(
+                s, cot_ref, grad_ref, flip_ref, hat_ref, scale_ref, gain_ref, bias_ref, input_ref, back, wide
+            )
+            if s == 0:
+                n_ref[...] = jnp.zeros_like(n_ref)
+                n_ref[0:1], n_ref[1:2] = weighted, plain
+            else:
+                n_ref[0:1] = n_ref[0:1] + weighted
+                n_ref[1:2] = n_ref[1:2] + plain
+                norm_pair = go(n_ref, n_pair, one_s.at[0], one_r.at[0], partner)
+        if s == 2:
             norm_pair.wait_recv()
             part = n_ref[...] + n_pair[...]
             n_y_src[...] = part
@@ -330,32 +421,6 @@
                 go(n_y_src, n_y.at[y], ny_s.at[i], ny_r.at[i], peer)
                 for i, peer in enumerate(y_peers)
             ]
-        if s == 1:
-            for copy in norm_y:
-                copy.wait_recv()
-            part = n_y[0]
-            for i in range(1, 8):
-                part = part + n_y[i]
-            n_x_src[...] = part
-            norm_x = go(n_x_src, n_x, one_s.at[1], one_r.at[1], across)
-        if s == 2:
-            norm_x.wait_recv()
-            part = n_x_src[...] + n_x[...]
-            n_z_src[...] = part
-            n_z[z] = part
-            norm_z = [
-                go(n_z_src, n_z.at[z], nz_s.at[i], nz_r.at[i], peer)
-                for i, peer in enumerate(z_peers)
-            ]
-        if s == 3:
-            for copy in norm_z:
-                copy.wait_recv()
-            part = n_z[0]
-            for i in range(1, 8):
-                part = part + n_z[i]
-            n_h_src[...] = part
-            norm_h = go(n_h_src, n_h, one_s.at[2], one_r.at[2], far)
-        edges.forward(s)
 
     totals = []
     for k in range(2):
@@ -367,6 +432,13 @@
     keep = jnp.where(x == 0, totals[0], totals[1])
     x_src[...] = jnp.where(x == 0, totals[1], totals[0])
     x_copy = go(x_src, x_dst, one_s.at[3], one_r.at[3], across)
+    for copy in norm_y:
+        copy.wait_recv()
+    part = n_y[0]
+    for i in range(1, 8):
+        part = part + n_y[i]
+    n_x_src[...] = part
+    norm_x = go(n_x_src, n_x, one_s.at[1], one_r.at[1], across)
     x_copy.wait_recv()
     value = keep + x_dst[...]
     for p in range(8):
@@ -376,6 +448,13 @@
         for i, peer in enumerate(z_peers)
     ]
     z_dst[z] = held[z]
+    norm_x.wait_recv()
+    part = n_x_src[...] + n_x[...]
+    n_z_src[...] = part
+    n_z[z] = part
+    norm_z = [
+        go(n_z_src, n_z.at[z], nz_s.at[i], nz_r.at[i], peer) for i, peer in enumerate(z_peers)
+    ]
     for copy in scatter:
         copy.wait_recv()
     part = z_dst[0]
@@ -383,8 +462,13 @@
         part = part + z_dst[i]
     h_src[...] = part
     h_copy = go(h_src, h_dst, one_s.at[4], one_r.at[4], far)
-    norm_h.wait_recv()
-    norm_ref[...] = n_h_src[...] + n_h[...]
+    for copy in norm_z:
+        copy.wait_recv()
+    part = n_z[0]
+    for i in range(1, 8):
+        part = part + n_z[i]
+    n_h_src[...] = part
+    norm_h = go(n_h_src, n_h, one_s.at[2], one_r.at[2], far)
     h_copy.wait_recv()
     part = h_src[...] + h_dst[...]
     z_src[...] = part
@@ -392,6 +476,8 @@
     spread = [
         go(z_src, out_ref.at[z], zg_s.at[i], zg_r.at[i], peer) for i, peer in enumerate(z_peers)
     ]
+    norm_h.wait_recv()
+    norm_ref[...] = (n_h_src[...] + n_h[...])[0:2]
     for copy in spread:
         copy.wait_recv()
     edges.finish()
@@ -399,21 +485,25 @@
         copy.wait_send()
 
 
-def reduce_gradient(gradient, norms, space):
+def reduce_gradient(gradient, space, *operands):
     f32, bf16 = jnp.float32, jnp.bfloat16
     dma, vmem = pltpu.SemaphoreType.DMA, pltpu.VMEM
-    small = vmem((8, 128), f32)
-    eight = vmem((8, 8, 128), f32)
+    small = vmem((8, 256), f32)
+    eight = vmem((8, 8, 256), f32)
     return pl.pallas_call(
         reduce_kernel,
         out_shape=(
             jax.ShapeDtypeStruct((8, 24, 128), f32),
-            jax.ShapeDtypeStruct((8, 128), f32),
+            jax.ShapeDtypeStruct((2, 256), f32),
+            jax.ShapeDtypeStruct(space.shape, space.dtype),
             jax.ShapeDtypeStruct(space.shape, space.dtype),
         ),
-        in_specs=[VMEM, VMEM, VMEM],
-        out_specs=(VMEM, VMEM, VMEM),
+        in_specs=[VMEM] * 9,
+        out_specs=(VMEM,) * 4,
         scratch_shapes=[
+            vmem((ROWS, 256), f32),
+            vmem((16, PITCH, 256), bf16),
+            small,
             vmem((8, 2, 96, 256), f32),
             vmem((2, 4, 2, 96, 256), bf16),
             vmem((2, 4, 2, 96, 256), bf16),
@@ -450,29 +540,10 @@
         ]
         + edge_scratch(space),
         compiler_params=pltpu.CompilerParams(
-            collective_id=1, has_side_effects=True, vmem_limit_bytes=18 * 2**20
+            collective_id=1, has_side_effects=True, vmem_limit_bytes=26 * 2**20
         ),
         name="reduce_gradient",
-    )(gradient.reshape(2, 8, 2, 96, 256), norms, space)
-
-
-PITCH = 48
-ROWS = 16 * PITCH
-TALL = ROWS + 2 * PITCH
-CHUNK = 2 * PITCH
-
-
-def group_mean(row):
-    rows = lax.broadcasted_iota(jnp.int32, (256, 256), 0) // 8
-    columns = lax.broadcasted_iota(jnp.int32, (256, 256), 1) // 8
-    same = (rows == columns).astype(jnp.float32)
-    total = jnp.dot(
-        jnp.broadcast_to(row, (8, 256)),
-        same,
-        precision=lax.Precision.HIGHEST,
-        preferred_element_type=jnp.float32,
-    )
-    return total[0:1] * (1.0 / (16 * 36 * 8))
+    )(gradient.reshape(2, 8, 2, 96, 256), space, *operands)
 
 
 def block_kernel(
@@ -483,17 +554,15 @@
     gain_ref,
     bias_ref,
     space_ref,
-    input_ref,
     g_ref,
-    norm_ref,
+    grad,
+    flip,
+    hat,
+    scale_ref,
     cot_pad,
     wide,
     tall,
-    hat,
-    back,
     act,
-    grad,
-    flip,
     space,
 ):
     f32, bf16 = jnp.float32, jnp.bfloat16
@@ -538,7 +607,6 @@
         return wide[pl.ds(i * 2, 2)].reshape(CHUNK, 256)
 
     zero = jnp.zeros((8, 256), f32)
-    inverse = []
     for f in range(2):
         wide[:, :36] = clip_ref[f].astype(f32)
         total = lax.fori_loop(0, 8, lambda i, carry: carry + folded(field(i)), zero)
@@ -551,7 +619,7 @@
         total = lax.fori_loop(0, 8, squares, zero)
         spread = group_mean(jnp.sum(total, axis=0, keepdims=True))
         scale = lax.rsqrt(spread + 1e-05)
-        inverse.append(scale)
+        scale_ref[f : f + 1] = scale
 
         def activate(i, carry):
             normed = jnp.where(inside, (field(i) - center) * scale, 0.0)
@@ -598,40 +666,6 @@
             total = term if total is None else total + term
         g_ref[i * 768 : (i + 1) * 768] = total
 
-    gain_sum, bias_sum = zero, zero
-    for f in range(2):
-        total = None
-        for i in range(3):
-            low = (2 - i) * PITCH
-            term = dot(grad[f, low : low + ROWS], flip[i * 768 : (i + 1) * 768])
-            total = term if total is None else total + term
-        back[...] = total
-
-        def pull(i, carry):
-            normed = hat[f, body(i)]
-            u = normed * gain + bias
-            gate = 1.0 / (1.0 + jnp.exp(-u))
-            down = jnp.where(inside, back[body(i)] * (gate * (1.0 + u * (1.0 - gate))), 0.0)
-            back[body(i)] = down
-            return carry[0] + folded(down), carry[1] + folded(down * normed)
-
-        plain, weighted = lax.fori_loop(0, 8, pull, (zero, zero))
-        bias_sum, gain_sum = bias_sum + plain, gain_sum + weighted
-        plain = group_mean(gain * jnp.sum(plain, axis=0, keepdims=True))
-        weighted = group_mean(gain * jnp.sum(weighted, axis=0, keepdims=True))
-        scale = inverse[f]
-
-        def finish(i, carry):
-            term = scale * (back[body(i)] * gain - plain - hat[f, body(i)] * weighted)
-            pair = cot_pad[f + 1, pl.ds(i * 2, 2)].reshape(CHUNK, 256)
-            result = (pair.astype(f32) + term).reshape(2, PITCH, 256)[:, :36]
-            input_ref[f, pl.ds(i * 2, 2)] = result.astype(bf16)
-            return carry
-
-        lax.fori_loop(0, 8, finish, 0)
-    norm_ref[0:1] = jnp.sum(gain_sum, axis=0, keepdims=True)
-    norm_ref[1:2] = jnp.sum(bias_sum, axis=0, keepdims=True)
-
 
 def block(clips, cotangent, edges, weights, gain, bias):
     f32, bf16 = jnp.float32, jnp.bfloat16
@@ -640,26 +674,24 @@
         block_kernel,
         out_shape=(
             jax.ShapeDtypeStruct(clips.shape, bf16),
-            jax.ShapeDtypeStruct(clips.shape, bf16),
             jax.ShapeDtypeStruct(weights.shape, f32),
+            jax.ShapeDtypeStruct((2, TALL, 768), bf16),
+            jax.ShapeDtypeStruct((2304, 256), bf16),
+            jax.ShapeDtypeStruct((2, ROWS, 256), f32),
             jax.ShapeDtypeStruct((2, 256), f32),
         ),
         in_specs=[VMEM] * 6,
-        out_specs=(VMEM,) * 4,
+        out_specs=(VMEM,) * 6,
         scratch_shapes=[
             vmem((4, 16, PITCH, 256), bf16),
             vmem((16, PITCH, 256), f32),
             vmem((TALL + 16, 256), f32),
-            vmem((2, ROWS, 256), f32),
-            vmem((ROWS, 256), f32),
             vmem((2, TALL, 768), bf16),
-            vmem((2, TALL, 768), bf16),
-            vmem((2304, 256), bf16),
             vmem((2, ROWS, 256), bf16),
         ],
-        compiler_params=pltpu.CompilerParams(vmem_limit_bytes=36 * 2**20),
+        compiler_params=pltpu.CompilerParams(vmem_limit_bytes=30 * 2**20),
         name="block",
-    )(clips, cotangent, edges, weights, gain.reshape(1, 256), bias.reshape(1, 256))
+    )(clips, cotangent, edges, weights, gain, bias)
 
 
 def shards(clips, cotangent, conv_master, first_moment, second_moment, norm_gain, norm_bias):
@@ -668,12 +700,11 @@
     clip, cot = clips[0], cotangent[0]
     rows, edges = gather_weights(conv_master.astype(jnp.bfloat16), cot)
     weights = rows.reshape(12 * channels, channels)
-    space, input_grad, local_gradient, norms = block(
-        clip, cot, edges, weights, norm_gain, norm_bias
+    gain, bias = norm_gain.reshape(1, channels), norm_bias.reshape(1, channels)
+    space, local_gradient, *saved = block(clip, cot, edges, weights, gain, bias)
+    pieces, norm_grads, around, input_grad = reduce_gradient(
+        local_gradient, space, cot, *saved, gain, bias
     )
-    norms = jnp.pad(norms.reshape(4, 128), ((0, 4), (0, 0)))
-    pieces, norm_sums, around = reduce_gradient(local_gradient, norms, space)
-    norm_grads = norm_sums[:4].reshape(2, channels)
     gradient = pieces.reshape(4, 2, 24, 128).transpose(0, 2, 1, 3).reshape(96, channels)
     t = lax.axis_index("tm")
     zero = jnp.zeros_like(around[:1])

time: 103 us -> 98.7 us (0.958)
  local copies, waits for them, and re-layouts: 8.44 us -> 4.88 us
  Pallas kernels: 91 us -> 89.9 us
    pallas_call x1, Pallas kernels: 14.9 us -> 9.11 us  [block(): pl.pallas_call(block_kernel, out_shape=(jax.ShapeDtypeStruct(clips.shape,...]
    pallas_call x1, Pallas kernels: 39.6 us -> 44.3 us  [reduce_gradient(): pl.pallas_call(reduce_kernel, out_shape=(jax.ShapeDtypeStruct((8, 24, 128...]
    unnamed x22 -> x19, local copies, waits for them, and re-layouts: 6.05 us -> 3.11 us
where the time goes in v4:
time: 98.7 us; the launch traced here: 98.5 us
  Pallas kernels  89.9 us (91%)
  local copies, waits for them, and re-layouts  4.88 us (5%)
  matrix products  2.12 us (2%)
    pallas_call x1, Pallas kernels, reduce_gradient(): pl.pallas_call(reduce_kernel, out_shape=(jax.ShapeDtypeStruct((8, 24, 128...  44.3 us
    pallas_call x1, Pallas kernels, gather_weights(): pl.pallas_call(gather_kernel, out_shape=(jax.ShapeDtypeStruct((32,) + row...  36.5 us
    pallas_call x1, Pallas kernels, block(): pl.pallas_call(block_kernel, out_shape=(jax.ShapeDtypeStruct(clips.shape,...  9.11 us
    unnamed x19, local copies, waits for them, and re-layouts  3.11 us
    dot_general x3, matrix products, shards(): jnp.einsum('fhwc,cd->fhwd', padded[frame_tap:frame_tap + 2], tap, preferr...  2.12 us

profile of v4, /device:TPU:8, one launch (start us, length us, event | category | flops | bytes accessed | tf_op | source)
XLA Modules:
  0.0 98.5 jit_solution(7088668988804230239)
XLA Ops:
  0.6 0.0 copy-start.4
  0.6 0.0 copy-start.2
  0.7 0.0 copy-start.3
  0.7 1.7 %copy_bitcast_fusion = (bf16[2,16,36,256]{3,2,1,0:T(8,128)(2,1)S(1)}, bf16[2,16,36,256]{3,2,1,0:T(8,128)(2,1)S(1)}) fusion(bf16[1,2,16,36,256]{4,2,3,1,0:T(8,128)(2,1)} %param.8, bf16[1,2,16,36,256]{4,2,3,1,0:T(8,128)(2,1)} %param.7), kind=kLoop, calls=%fused_computation.12 | loop fusion | bytes 2359296 | tf_op jit(solution)/shard_map/squeeze | solution.py:700
  2.4 0.0 copy-done.4
  2.4 36.5 %gather_weights.1 = (bf16[32,96,256]{2,1,0:T(8,128)(2,1)S(1)}, bf16[2,16,36,256]{3,2,1,0:T(8,128)(2,1)S(1)}) custom-call(bf16[96,256]{1,0:T(8,128)(2,1)S(1)} %convert_element_type.10.w_ref, bf16[2,16,36,256]{3,2,1,0:T(8,128)(2,1)S(1)} %get-tuple-element.41.cot_ref), custom_call_target="tpu_custom_call" | custom-call | tf_op jit(solution)/shard_map/gather_weights/pallas_call | solution.py:199
  38.9 0.0 copy-done.2
  38.9 0.0 copy-done.3
  38.9 9.1 %block.1 = (bf16[2,16,36,256]{3,2,1,0:T(8,128)(2,1)S(1)}, f32[3072,256]{1,0:T(8,128)S(1)}, bf16[2,864,768]{2,1,0:T(8,128)(2,1)S(1)}, bf16[2304,256]{1,0:T(8,128)...) custom-call(bf16[2,16,36,256]{3,2,1,0:T(8,128)(2,1)S(1)} %get-tuple-element.42.clip_ref, ...), custom_call_target="tpu_custom_call" | custom-call | tf_op jit(solution)/shard_map/block/pallas_call | solution.py:673
  48.0 44.3 %reduce_gradient.1 = (f32[8,24,128]{2,1,0:T(8,128)S(1)}, f32[2,256]{1,0:T(2,128)S(1)}, bf16[2,16,36,256]{3,2,1,0:T(8,128)(2,1)S(1)}, bf16[2,16,36,256]{3,2,1,0:T(8,128)(2,1)S(1)}) custom-call(f32[2,8,2,96,256]{4,3,2,1,0:T(8,128)S(1)} %bitcast.41, bf16[2,16,36,256]{3,2,1,0:T(8,128)(2,1)S(1)} %get-tuple-element.21.space_ref, ...), custom_call_target="tpu_custom_call" | custom-call | tf_op jit(solution)/shard_map/reduce_gradient/pallas_call | solution.py:493
  92.3 0.0 copy-start
  92.3 0.6 copy-done
  93.0 1.4 %convolution_add_fusion.1 = f32[2,16,36,256]{3,2,1,0:T(8,128)S(1)} fusion(bf16[2,16,36,256]{3,2,1,0:T(8,128)(2,1)S(1)} %get-tuple-element.21.space_ref, bf16[1,16,36,256]{3,2,1,0:T(8,128)(2,1)S(1)} %get-tuple-element.39, bf16[3072,256]{1,0:T(8,128)(2,1)S(1)} %bitcast.43, bf16[1,2,16,36,256]{4,2,3,1,0:T(8,128)(2,1)} %param.7), kind=kOutput, calls=%fused_computation.2 | convolution fusion | flops 153354240 | bytes 2883584 | tf_op jit(solution)/shard_map/fhwc,cd->fhwd/dot_general | solution.py:721
  94.4 0.3 fusion.6
  94.8 0.3 fusion.2
  95.1 0.0 copy-start.1
  95.2 0.0 copy-start.5
  95.2 0.0 copy-start.6
  95.2 0.0 copy-start.7
  95.2 0.9 copy.16
  96.1 0.9 copy.17
  97.0 0.0 copy-done.1
  97.0 0.1 copy.15
  97.1 0.0 copy-done.5
  97.1 0.0 copy-done.6
  97.1 0.0 copy-done.7
  97.1 0.7 multiply_subtract_fusion
  97.9 0.6 copy.31
  (2 shorter events, 0.1 us)
Async XLA Ops:
  0.6 1.8 %copy-start.4 = (f32[96,256]{1,0:T(8,128)S(1)}, f32[96,256]{1,0:T(8,128)}, u32[]{:S(2)}) copy-start(f32[96,256]{1,0:T(8,128)} %param.9) | copy-start | bytes 294916
  0.6 38.3 %copy-start.2 = (f32[256]{0:T(256)S(1)}, f32[256]{0:T(256)}, u32[]{:S(2)}) copy-start(f32[256]{0:T(256)} %param.12) | copy-start | bytes 3076
  0.7 38.3 %copy-start.3 = (f32[256]{0:T(256)S(1)}, f32[256]{0:T(256)}, u32[]{:S(2)}) copy-start(f32[256]{0:T(256)} %param.13) | copy-start | bytes 3076
  92.3 0.6 copy-start
  95.1 1.9 %copy-start.1 = (f32[8,24,128]{2,1,0:T(8,128)S(1)}, f32[8,24,128]{2,1,0:T(8,128)}, u32[]{:S(2)}) copy-start(f32[8,24,128]{2,1,0:T(8,128)} %copy-done) | copy-start | bytes 294916
  95.2 2.0 %copy-start.5 = (f32[96,256]{1,0:T(8,128)S(1)}, f32[96,256]{1,0:T(8,128)}, u32[]{:S(2)}) copy-start(f32[96,256]{1,0:T(8,128)} %param.9) | copy-start | bytes 294916
  95.2 1.9 %copy-start.6 = (f32[96,256]{1,0:T(8,128)S(1)}, f32[96,256]{1,0:T(8,128)}, u32[]{:S(2)}) copy-start(f32[96,256]{1,0:T(8,128)} %param.10) | copy-start | bytes 294916
  95.2 1.9 %copy-start.7 = (f32[96,256]{1,0:T(8,128)S(1)}, f32[96,256]{1,0:T(8,128)}, u32[]{:S(2)}) copy-start(f32[96,256]{1,0:T(8,128)} %param.11) | copy-start | bytes 294916

commit v5 on v4

--- a/solution.py
+++ b/solution.py
@@ -118,11 +118,91 @@
     return [pltpu.VMEM(frames.shape, frames.dtype)] + [dma((2, 4))] * 4
 
 
+PITCH = 48
+ROWS = 16 * PITCH
+TALL = ROWS + 2 * PITCH
+CHUNK = 2 * PITCH
+
+
+def group_mean(row):
+    rows = lax.broadcasted_iota(jnp.int32, (256, 256), 0) // 8
+    columns = lax.broadcasted_iota(jnp.int32, (256, 256), 1) // 8
+    same = (rows == columns).astype(jnp.float32)
+    total = jnp.dot(
+        jnp.broadcast_to(row, (8, 256)),
+        same,
+        precision=lax.Precision.HIGHEST,
+        preferred_element_type=jnp.float32,
+    )
+    return total[0:1] * (1.0 / (16 * 36 * 8))
+
+
+def shift(tall, target, f):
+    for j in range(3):
+        for start in range(0, TALL, CHUNK):
+            target[f, start : start + CHUNK, j * 256 : (j + 1) * 256] = tall[
+                start + 7 + j : start + 7 + j + CHUNK
+            ].astype(jnp.bfloat16)
+
+
+def norm_forward(f, clip_ref, gain_ref, bias_ref, act, hat, scale_ref, wide, tall):
+    f32 = jnp.float32
+    gain, bias = gain_ref[...], bias_ref[...]
+    inside = (lax.broadcasted_iota(jnp.int32, (2, PITCH, 256), 1) < 36).reshape(CHUNK, 256)
+    zero = jnp.zeros((8, 256), f32)
+    wide[...] = jnp.zeros_like(wide)
+    tall[...] = jnp.zeros_like(tall)
+    wide[:, :36] = clip_ref[f].astype(f32)
+
+    def body(start):
+        return pl.ds(pl.multiple_of(start * CHUNK, CHUNK), CHUNK)
+
+    def above(start):
+        return pl.ds(pl.multiple_of(start * CHUNK + PITCH + 8, 8), CHUNK)
+
+    def folded(value):
+        return jnp.sum(value.reshape(CHUNK // 8, 8, 256), axis=0)
+
+    def field(i):
+        return wide[pl.ds(i * 2, 2)].reshape(CHUNK, 256)
+
+    total = lax.fori_loop(0, 8, lambda i, carry: carry + folded(field(i)), zero)
+    center = group_mean(jnp.sum(total, axis=0, keepdims=True))
+
+    def squares(i, carry):
+        value = jnp.where(inside, field(i) - center, 0.0)
+        return carry + folded(value * value)
+
+    total = lax.fori_loop(0, 8, squares, zero)
+    spread = group_mean(jnp.sum(total, axis=0, keepdims=True))
+    scale = lax.rsqrt(spread + 1e-05)
+    scale_ref[f : f + 1] = scale
+
+    def activate(i, carry):
+        normed = jnp.where(inside, (field(i) - center) * scale, 0.0)
+        hat[f, body(i)] = normed
+        u = normed * gain + bias
+        value = jnp.where(inside, u / (1.0 + jnp.exp(-u)), 0.0)
+        tall[above(i)] = value
+        return carry
+
+    lax.fori_loop(0, 8, activate, 0)
+    shift(tall, act, f)
+
+
 def gather_kernel(
     w_ref,
     cot_ref,
+    clip_ref,
+    gain_ref,
+    bias_ref,
     out_ref,
     edge_ref,
+    act_ref,
+    hat_ref,
+    scale_ref,
+    wide,
+    tall,
     ring_send,
     ring_recv,
     pair_send,
@@ -159,6 +239,8 @@
         copies[d, 0] = hop(w_ref, d, 0, 0)
     pass_on(w_ref, 0, 0)
     edges.start()
+    saved = clip_ref, gain_ref, bias_ref, act_ref, hat_ref, scale_ref, wide, tall
+    norm_forward(0, *saved)
     out_ref[mine] = w_ref[...]
     x_copy.wait_recv()
     other = out_ref.at[owner(1 - x, y, c)]
@@ -177,6 +259,8 @@
                     copies[d, k] = hop(block, d, s, k)
                 pass_on(block, k, offset)
         edges.forward(s - 1)
+        if s == 1:
+            norm_forward(1, *saved)
     x_copy.wait_send()
     for copy in started:
         copy.wait_send()
@@ -194,17 +278,22 @@
     edges.finish()
 
 
-def gather_weights(rows, cotangent):
+def gather_weights(rows, cotangent, clips, gain, bias):
     dma = pltpu.SemaphoreType.DMA
     return pl.pallas_call(
         gather_kernel,
         out_shape=(
             jax.ShapeDtypeStruct((32,) + rows.shape, rows.dtype),
             jax.ShapeDtypeStruct(cotangent.shape, cotangent.dtype),
+            jax.ShapeDtypeStruct((2, TALL, 768), jnp.bfloat16),
+            jax.ShapeDtypeStruct((2, ROWS, 256), jnp.float32),
+            jax.ShapeDtypeStruct((2, 256), jnp.float32),
         ),
-        in_specs=[VMEM, VMEM],
-        out_specs=(VMEM, VMEM),
+        in_specs=[VMEM] * 5,
+        out_specs=(VMEM,) * 5,
         scratch_shapes=[
+            pltpu.VMEM((16, PITCH, 256), jnp.float32),
+            pltpu.VMEM((TALL + 16, 256), jnp.float32),
             dma((2, 4, 2)),
             dma((2, 4, 2)),
             dma((16,)),
@@ -214,29 +303,10 @@
         ]
         + edge_scratch(cotangent),
         compiler_params=pltpu.CompilerParams(
-            collective_id=0, has_side_effects=True, vmem_limit_bytes=10 * 2**20
+            collective_id=0, has_side_effects=True, vmem_limit_bytes=18 * 2**20
         ),
         name="gather_weights",
-    )(rows, cotangent)
-
-
-PITCH = 48
-ROWS = 16 * PITCH
-TALL = ROWS + 2 * PITCH
-CHUNK = 2 * PITCH
-
-
-def group_mean(row):
-    rows = lax.broadcasted_iota(jnp.int32, (256, 256), 0) // 8
-    columns = lax.broadcasted_iota(jnp.int32, (256, 256), 1) // 8
-    same = (rows == columns).astype(jnp.float32)
-    total = jnp.dot(
-        jnp.broadcast_to(row, (8, 256)),
-        same,
-        precision=lax.Precision.HIGHEST,
-        preferred_element_type=jnp.float32,
-    )
-    return total[0:1] * (1.0 / (16 * 36 * 8))
+    )(rows, cotangent, clips, gain, bias)
 
 
 def pull_back(
@@ -547,42 +617,25 @@
 
 
 def block_kernel(
-    clip_ref,
+    act,
     cot_ref,
     edge_ref,
     w_ref,
-    gain_ref,
-    bias_ref,
     space_ref,
     g_ref,
     grad,
     flip,
-    hat,
-    scale_ref,
     cot_pad,
-    wide,
     tall,
-    act,
     space,
 ):
     f32, bf16 = jnp.float32, jnp.bfloat16
     t = lax.axis_index("tm")
-    gain, bias = gain_ref[...], bias_ref[...]
-    inside = (lax.broadcasted_iota(jnp.int32, (2, PITCH, 256), 1) < 36).reshape(CHUNK, 256)
-
     def dot(a, b, contract=(1, 0)):
         dims = (((contract[0],), (contract[1],)), ((), ()))
         return lax.dot_general(a, b, dims, preferred_element_type=f32)
 
-    def shift(target, f):
-        for j in range(3):
-            for start in range(0, TALL, CHUNK):
-                target[f, start : start + CHUNK, j * 256 : (j + 1) * 256] = tall[
-                    start + 7 + j : start + 7 + j + CHUNK
-                ].astype(bf16)
-
     cot_pad[...] = jnp.zeros_like(cot_pad)
-    wide[...] = jnp.zeros_like(wide)
     tall[...] = jnp.zeros_like(tall)
     cot_pad[0, :, :36] = jnp.where(t == 0, 0.0, edge_ref[0].astype(f32)).astype(bf16)
     cot_pad[1, :, :36] = cot_ref[0]
@@ -594,44 +647,6 @@
             slot = 3 * i + 2 - j
             flip[slot * 256 : (slot + 1) * 256] = w_ref[tap * 256 : (tap + 1) * 256].T
 
-    def body(start):
-        return pl.ds(pl.multiple_of(start * CHUNK, CHUNK), CHUNK)
-
-    def above(start):
-        return pl.ds(pl.multiple_of(start * CHUNK + PITCH + 8, 8), CHUNK)
-
-    def folded(value):
-        return jnp.sum(value.reshape(CHUNK // 8, 8, 256), axis=0)
-
-    def field(i):
-        return wide[pl.ds(i * 2, 2)].reshape(CHUNK, 256)
-
-    zero = jnp.zeros((8, 256), f32)
-    for f in range(2):
-        wide[:, :36] = clip_ref[f].astype(f32)
-        total = lax.fori_loop(0, 8, lambda i, carry: carry + folded(field(i)), zero)
-        center = group_mean(jnp.sum(total, axis=0, keepdims=True))
-
-        def squares(i, carry):
-            value = jnp.where(inside, field(i) - center, 0.0)
-            return carry + folded(value * value)
-
-        total = lax.fori_loop(0, 8, squares, zero)
-        spread = group_mean(jnp.sum(total, axis=0, keepdims=True))
-        scale = lax.rsqrt(spread + 1e-05)
-        scale_ref[f : f + 1] = scale
-
-        def activate(i, carry):
-            normed = jnp.where(inside, (field(i) - center) * scale, 0.0)
-            hat[f, body(i)] = normed
-            u = normed * gain + bias
-            value = jnp.where(inside, u / (1.0 + jnp.exp(-u)), 0.0)
-            tall[above(i)] = value
-            return carry
-
-        lax.fori_loop(0, 8, activate, 0)
-        shift(act, f)
-
     for f in range(2):
         total = dot(act[f, 0:ROWS], w_ref[0:768])
         for i in range(1, 3):
@@ -647,7 +662,7 @@
             term = dot(cot_pad[f + 2 - k].reshape(ROWS, 256), tap, (1, 1))
             total = term if total is None else total + term
         tall[PITCH + 8 : PITCH + 8 + ROWS] = total.astype(bf16).astype(f32)
-        shift(grad, f)
+        shift(tall, grad, f)
 
     for k in range(3):
         total = None
@@ -667,43 +682,41 @@
         g_ref[i * 768 : (i + 1) * 768] = total
 
 
-def block(clips, cotangent, edges, weights, gain, bias):
+def block(act, cotangent, edges, weights):
     f32, bf16 = jnp.float32, jnp.bfloat16
     vmem = pltpu.VMEM
     return pl.pallas_call(
         block_kernel,
         out_shape=(
-            jax.ShapeDtypeStruct(clips.shape, bf16),
+            jax.ShapeDtypeStruct(cotangent.shape, bf16),
             jax.ShapeDtypeStruct(weights.shape, f32),
             jax.ShapeDtypeStruct((2, TALL, 768), bf16),
             jax.ShapeDtypeStruct((2304, 256), bf16),
-            jax.ShapeDtypeStruct((2, ROWS, 256), f32),
-            jax.ShapeDtypeStruct((2, 256), f32),
         ),
-        in_specs=[VMEM] * 6,
-        out_specs=(VMEM,) * 6,
+        in_specs=[VMEM] * 4,
+        out_specs=(VMEM,) * 4,
         scratch_shapes=[
             vmem((4, 16, PITCH, 256), bf16),
-            vmem((16, PITCH, 256), f32),
             vmem((TALL + 16, 256), f32),
-            vmem((2, TALL, 768), bf16),
             vmem((2, ROWS, 256), bf16),
         ],
         compiler_params=pltpu.CompilerParams(vmem_limit_bytes=30 * 2**20),
         name="block",
-    )(clips, cotangent, edges, weights, gain, bias)
+    )(act, cotangent, edges, weights)
 
 
 def shards(clips, cotangent, conv_master, first_moment, second_moment, norm_gain, norm_bias):
     f32 = jnp.float32
     channels = clips.shape[-1]
     clip, cot = clips[0], cotangent[0]
-    rows, edges = gather_weights(conv_master.astype(jnp.bfloat16), cot)
+    gain, bias = norm_gain.reshape(1, channels), norm_bias.reshape(1, channels)
+    rows, edges, act, hat, scale = gather_weights(
+        conv_master.astype(jnp.bfloat16), cot, clip, gain, bias
+    )
     weights = rows.reshape(12 * channels, channels)
-    gain, bias = norm_gain.reshape(1, channels), norm_bias.reshape(1, channels)
-    space, local_gradient, *saved = block(clip, cot, edges, weights, gain, bias)
+    space, local_gradient, grad, flip = block(act, cot, edges, weights)
     pieces, norm_grads, around, input_grad = reduce_gradient(
-        local_gradient, space, cot, *saved, gain, bias
+        local_gradient, space, cot, grad, flip, hat, scale, gain, bias
     )
     gradient = pieces.reshape(4, 2, 24, 128).transpose(0, 2, 1, 3).reshape(96, channels)
     t = lax.axis_index("tm")

time: 98.7 us -> 96.7 us (0.980)
  the two profiles are of different devices: /device:TPU:8 before, /device:TPU:16 now
where the time goes in v5:
time: 96.7 us; the launch traced here: 96.5 us
  Pallas kernels  87.9 us (91%)
  local copies, waits for them, and re-layouts  4.87 us (5%)
  matrix products  2.13 us (2%)
    pallas_call x1, Pallas kernels, reduce_gradient(): pl.pallas_call(reduce_kernel, out_shape=(jax.ShapeDtypeStruct((8, 24, 128...  47 us
    pallas_call x1, Pallas kernels, gather_weights(): pl.pallas_call(gather_kernel, out_shape=(jax.ShapeDtypeStruct((32,) + row...  35.3 us
    pallas_call x1, Pallas kernels, block(): pl.pallas_call(block_kernel, out_shape=(jax.ShapeDtypeStruct(cotangent.sh...  5.67 us
    unnamed x19, local copies, waits for them, and re-layouts  3.11 us
    dot_general x3, matrix products, shards(): jnp.einsum('fhwc,cd->fhwd', padded[frame_tap:frame_tap + 2], tap, preferr...  2.13 us

profile of v5, /device:TPU:16, one launch (start us, length us, event | category | flops | bytes accessed | tf_op | source)
XLA Modules:
  0.0 96.5 jit_solution(3505309063906213230)
XLA Ops:
  0.6 0.0 copy-start.2
  0.6 0.0 copy-start.3
  0.7 0.0 copy-start.4
  0.7 1.7 %copy_bitcast_fusion = (bf16[2,16,36,256]{3,2,1,0:T(8,128)(2,1)S(1)}, bf16[2,16,36,256]{3,2,1,0:T(8,128)(2,1)S(1)}) fusion(bf16[1,2,16,36,256]{4,2,3,1,0:T(8,128)(2,1)} %param.8, bf16[1,2,16,36,256]{4,2,3,1,0:T(8,128)(2,1)} %param.7), kind=kLoop, calls=%fused_computation.12 | loop fusion | bytes 2359296 | tf_op jit(solution)/shard_map/squeeze | solution.py:711
  2.4 0.0 copy-done.4
  2.4 0.0 copy-done.2
  2.4 0.0 copy-done.3
  2.4 35.3 %gather_weights.1 = (bf16[32,96,256]{2,1,0:T(8,128)(2,1)S(1)}, bf16[2,16,36,256]{3,2,1,0:T(8,128)(2,1)S(1)}, bf16[2,864,768]{2,1,0:T(8,128)(2,1)S(1)}, f32[2,768,256]{2,1,0:T(8,128)S(1)}, f32[2,256]{1,0:T(2,128)S(1)}) custom-call(bf16[96,256]{1,0:T(8,128)(2,1)S(1)} %convert_element_type.10.w_ref, bf16[2,16,36,256]{3,2,1,0:T(8,128)(2,1)S(1)} %get-tuple-element.43.cot_ref, ...), custom_call_target="tpu_custom_call" | custom-call | tf_op jit(solution)/shard_map/gather_weights/pallas_call | solution.py:283
  37.7 5.7 %block.1 = (bf16[2,16,36,256]{3,2,1,0:T(8,128)(2,1)S(1)}, f32[3072,256]{1,0:T(8,128)S(1)}, bf16[2,864,768]{2,1,0:T(8,128)(2,1)S(1)}, bf16[2304,256]{1,0:T(8,128)(2,1)S(1)}) custom-call(bf16[2,864,768]{2,1,0:T(8,128)(2,1)S(1)} %get-tuple-element.19.act, bf16[2,16,36,256]{3,2,1,0:T(8,128)(2,1)S(1)} %get-tuple-element.43.cot_ref, ...), custom_call_target="tpu_custom_call" | custom-call | tf_op jit(solution)/shard_map/block/pallas_call | solution.py:688
  43.4 47.0 %reduce_gradient.1 = (f32[8,24,128]{2,1,0:T(8,128)S(1)}, f32[2,256]{1,0:T(2,128)S(1)}, bf16[2,16,36,256]{3,2,1,0:T(8,128)(2,1)S(1)}, bf16[2,16,36,256]{3,2,1,0:T(8,128)(2,1)S(1)}) custom-call(f32[2,8,2,96,256]{4,3,2,1,0:T(8,128)S(1)} %bitcast.41, bf16[2,16,36,256]{3,2,1,0:T(8,128)(2,1)S(1)} %get-tuple-element.23.space_ref, ...), custom_call_target="tpu_custom_call" | custom-call | tf_op jit(solution)/shard_map/reduce_gradient/pallas_call | solution.py:563
  90.4 0.0 copy-start
  90.4 0.6 copy-done
  91.1 1.4 %convolution_add_fusion.1 = f32[2,16,36,256]{3,2,1,0:T(8,128)S(1)} fusion(bf16[2,16,36,256]{3,2,1,0:T(8,128)(2,1)S(1)} %get-tuple-element.23.space_ref, bf16[1,16,36,256]{3,2,1,0:T(8,128)(2,1)S(1)} %get-tuple-element.41, bf16[3072,256]{1,0:T(8,128)(2,1)S(1)} %bitcast.43, bf16[1,2,16,36,256]{4,2,3,1,0:T(8,128)(2,1)} %param.7), kind=kOutput, calls=%fused_computation.2 | convolution fusion | flops 153354240 | bytes 2883584 | tf_op jit(solution)/shard_map/fhwc,cd->fhwd/dot_general | solution.py:734
  92.5 0.3 fusion.6
  92.9 0.3 fusion.2
  93.2 0.0 copy-start.1
  93.2 0.0 copy-start.5
  93.2 0.0 copy-start.6
  93.2 0.0 copy-start.7
  93.3 0.9 copy.16
  94.2 0.9 copy.17
  95.1 0.0 copy-done.1
  95.1 0.1 copy.15
  95.2 0.0 copy-done.5
  95.2 0.0 copy-done.6
  95.2 0.0 copy-done.7
  95.2 0.7 multiply_subtract_fusion
  95.9 0.6 copy.31
  (2 shorter events, 0.1 us)
Async XLA Ops:
  0.6 1.8 %copy-start.2 = (f32[256]{0:T(256)S(1)}, f32[256]{0:T(256)}, u32[]{:S(2)}) copy-start(f32[256]{0:T(256)} %param.12) | copy-start | bytes 3076
  0.6 1.8 %copy-start.3 = (f32[256]{0:T(256)S(1)}, f32[256]{0:T(256)}, u32[]{:S(2)}) copy-start(f32[256]{0:T(256)} %param.13) | copy-start | bytes 3076
  0.7 1.7 %copy-start.4 = (f32[96,256]{1,0:T(8,128)S(1)}, f32[96,256]{1,0:T(8,128)}, u32[]{:S(2)}) copy-start(f32[96,256]{1,0:T(8,128)} %param.9) | copy-start | bytes 294916
  90.4 0.6 copy-start
  93.2 1.9 %copy-start.1 = (f32[8,24,128]{2,1,0:T(8,128)S(1)}, f32[8,24,128]{2,1,0:T(8,128)}, u32[]{:S(2)}) copy-start(f32[8,24,128]{2,1,0:T(8,128)} %copy-done) | copy-start | bytes 294916
  93.2 2.0 %copy-start.5 = (f32[96,256]{1,0:T(8,128)S(1)}, f32[96,256]{1,0:T(8,128)}, u32[]{:S(2)}) copy-start(f32[96,256]{1,0:T(8,128)} %param.9) | copy-start | bytes 294916
  93.2 1.9 %copy-start.6 = (f32[96,256]{1,0:T(8,128)S(1)}, f32[96,256]{1,0:T(8,128)}, u32[]{:S(2)}) copy-start(f32[96,256]{1,0:T(8,128)} %param.10) | copy-start | bytes 294916
  93.2 1.9 %copy-start.7 = (f32[96,256]{1,0:T(8,128)S(1)}, f32[96,256]{1,0:T(8,128)}, u32[]{:S(2)}) copy-start(f32[96,256]{1,0:T(8,128)} %param.11) | copy-start | bytes 294916
